TPU v7x, 256 devices: a whole 4x4x8 slice. The times are simulated.
256 devices in a mesh: row: 32 (over y, z), col: 8 (over x, core).
Axes of the slice: x: 4, y: 4, z: 8, core: 2. Of those that a mesh axis runs over, the one named last changes fastest.
Arguments:
- trailing_matrix: float32 [8192, 8192], P('row', 'col'), may hold values from -24 to 1024, as said below
- rhs_block: float32 [8192, 128], P('row'), may hold values from -144 to 144
Outputs:
- factored: float32 [8192, 8192], P('row', 'col')
- solved_rhs: float32 [8192, 128], P('row')
Inputs may be any that keep to these rules, and one draw needn't show every extreme that they name: `trailing_matrix`: symmetric in logical order; its leading 2 * 256 by 512 logical block is positive definite.
All inputs are finite; a program needn't handle non-finite values.
Results may differ from a plain program's by a relative error of at most 0.00011.
Values sent between devices are 32-bit elements; how exact they have to be, the bound alone decides.
No kernel may reach another device: no remote copies, remote signals or barrier semaphores. Data moves between devices by JAX's collectives and lax.ppermute only.
A program may use at most 64 MiB of HBM per device.

v0:
```python
import jax
import jax.numpy as jnp
from jax import lax
from jax.experimental import pallas as pl
from jax.experimental.pallas import tpu as pltpu
from jax.sharding import Mesh
from jax.sharding import PartitionSpec as P


NB = 256
BLK = 128
SUB = 8
AXES = ("y", "z", "x", "core")
NY, NZ, NX, NK = 4, 8, 4, 2


highest = lax.Precision.HIGHEST


def fid(y, z, x, k):
    return ((y % NY * NZ + z % NZ) * NX + x % NX) * NK + k


EVERY = [
    (y, z, x, k) for y in range(NY) for z in range(NZ) for x in range(NX) for k in range(NK)
]


def shift(dy=0, dz=0, dx=0):
    return [(fid(*p), fid(p[0] + dy, p[1] + dz, p[2] + dx, p[3])) for p in EVERY]


SWAP = [(fid(y, z, x, k), fid(y, z, x, 1 - k)) for y, z, x, k in EVERY]

RING4 = [[(0, 1)], [(0, 3), (1, 2)]]
RING8 = [[(0, 1), (1, 0)], [(0, 6), (1, 3)], [(0, 7), (1, 2), (6, 5), (3, 4)]]


def plane_rounds(order, core):
    have = {"y": [0], "z": [0, 1]}
    rounds = []
    for axis in order:
        for pairs in RING4 if axis == "y" else RING8:
            links = []
            for src, dst in pairs:
                for u in have["z" if axis == "y" else "y"]:
                    for x in range(NX):
                        if axis == "y":
                            links.append((fid(src, u, x, core), fid(dst, u, x, core)))
                        else:
                            links.append((fid(u, src, x, core), fid(u, dst, x, core)))
            have[axis] = sorted(set(have[axis] + [dst for _, dst in pairs]))
            rounds.append(links)
    return rounds


LEAD_ROUNDS = [p + q for p, q in zip(plane_rounds("zy", 0), plane_rounds("yz", 1))]


def send(value, pairs):
    return lax.ppermute(value, AXES, pairs)


def after(value, *others):
    return lax.optimization_barrier((value,) + others)[0]


def eliminate(rows, inv):
    n = len(rows)
    sub = lax.broadcasted_iota(jnp.int32, (SUB, BLK), 0)
    upper, lower_inv = [], []
    for k in range(n):
        D, F = rows[k], inv[k]
        col = [jnp.broadcast_to(D[:, SUB * k + s : SUB * k + s + 1], (SUB, BLK)) for s in range(SUB)]
        recip, cross, d_row, f_row = [], {}, [], []
        scale = jnp.zeros((SUB, BLK), jnp.float32)
        for s in range(SUB):
            pivot = jnp.broadcast_to(col[s][s : s + 1, :], (SUB, BLK))
            recip.append(1.0 / pivot)
            scale = jnp.where(sub == s, lax.rsqrt(pivot), scale)
            mult = jnp.where(sub > s, col[s] * recip[s], 0.0)
            for t in range(s + 1, SUB):
                cross[s, t] = jnp.broadcast_to(col[t][s : s + 1, :], (SUB, BLK))
                col[t] = col[t] - mult * cross[s, t]
            d_row.append(jnp.broadcast_to(D[s : s + 1, :], (SUB, BLK)))
            f_row.append(jnp.broadcast_to(F[s : s + 1, :], (SUB, BLK)))
            if s < SUB - 1:
                D = D - mult * d_row[s]
                F = F - mult * f_row[s]
        upper.append(D * scale)
        lower_inv.append(F * scale)
        for i in range(k + 1, n):
            part = [
                jnp.broadcast_to(rows[i][:, SUB * k + s : SUB * k + s + 1], (SUB, BLK))
                for s in range(SUB)
            ]
            p, q = rows[i], inv[i]
            for s in range(SUB):
                mult = part[s] * recip[s]
                for t in range(s + 1, SUB):
                    part[t] = part[t] - mult * cross[s, t]
                p = p - mult * d_row[s]
                q = q - mult * f_row[s]
            rows[i], inv[i] = p, q
    return upper, lower_inv


def factor_block(block):
    n = BLK // SUB
    rows = [block[SUB * i : SUB * i + SUB, :] for i in range(n)]
    r = lax.broadcasted_iota(jnp.int32, (SUB, BLK), 0)
    c = lax.broadcasted_iota(jnp.int32, (SUB, BLK), 1)
    inv = [jnp.where(r + SUB * i == c, 1.0, 0.0).astype(jnp.float32) for i in range(n)]
    upper, lower_inv = eliminate(rows, inv)
    upper = [jnp.where(c >= r + SUB * i, upper[i], 0.0) for i in range(n)]
    return jnp.concatenate(upper, 0), jnp.concatenate(lower_inv, 0)


def mm(a, b):
    return lax.dot_general(a, b, (((1,), (0,)), ((), ())), precision=highest,
                           preferred_element_type=jnp.float32)


def mm_t(a, b):
    return lax.dot_general(a, b, (((1,), (1,)), ((), ())), precision=highest,
                           preferred_element_type=jnp.float32)


def split(v):
    high = v.astype(jnp.bfloat16)
    return high, (v - high.astype(jnp.float32)).astype(jnp.bfloat16)


def dot3(a, b, transposed=False):
    dims = (((1,), (1 if transposed else 0,)), ((), ()))
    prod = lambda p, q: lax.dot_general(p, q, dims, preferred_element_type=jnp.float32)
    return prod(a[0], b[0]) + (prod(a[0], b[1]) + prod(a[1], b[0]))


def unpack(x, core, mine_ref, other_ref, rows, plane, out_ref):
    size = rows.stop - rows.start
    for p in range(NX):
        at = lax.rem(p - x + NX, NX)
        mine, other = mine_ref[at, rows], other_ref[at, rows]
        out_ref[p * size : (p + 1) * size] = jnp.where(core == plane, mine, other)


def first_half0_kernel(where_ref, mine_ref, other_ref, ua_ref, la_ref, ub_ref, s_ref, blocks_ref):
    unpack(where_ref[3], where_ref[4], mine_ref, other_ref, slice(0, 96), 0, blocks_ref)
    first_half_kernel(blocks_ref, ua_ref, la_ref, ub_ref, s_ref)


def first_half_kernel(blocks_ref, ua_ref, la_ref, ub_ref, s_ref):
    ua, la = factor_block(blocks_ref[:BLK])
    ub = mm(la, blocks_ref[BLK : 2 * BLK])
    ua_ref[...] = ua
    la_ref[...] = la
    ub_ref[...] = ub
    s_ref[...] = blocks_ref[2 * BLK :] - mm(ub.T, ub)


def second_half(ua, la, ub, s, u_ref, inv_ref):
    uc, lc = factor_block(s)
    zero = jnp.zeros((BLK, BLK), jnp.float32)
    u_ref[:BLK, :BLK] = ua
    u_ref[:BLK, BLK:] = ub
    u_ref[BLK:, :BLK] = zero
    u_ref[BLK:, BLK:] = uc
    inv_ref[:BLK, :BLK] = la
    inv_ref[:BLK, BLK:] = zero
    inv_ref[BLK:, :BLK] = -mm(lc, mm(ub.T, la))
    inv_ref[BLK:, BLK:] = lc


def second_half0_kernel(
    where_ref, mine_ref, other_ref, ua_ref, la_ref, ub_ref, s_ref,
    u_ref, inv_ref, u01_ref, s11_ref, y0_ref, rest_ref,
    top2_ref, right_ref, a11_ref, be0_ref, be1_ref, b0_ref, b1_ref,
):
    x, core = where_ref[3], where_ref[4]
    unpack(x, core, mine_ref, other_ref, slice(96, 160), 0, top2_ref)
    unpack(x, core, mine_ref, other_ref, slice(96, 160), 1, right_ref)
    unpack(x, core, mine_ref, other_ref, slice(0, 96), 1, a11_ref)
    unpack(x, core, mine_ref, other_ref, slice(160, 224), 0, be0_ref)
    unpack(x, core, mine_ref, other_ref, slice(160, 224), 1, be1_ref)
    for p in range(NX):
        for k, ref in enumerate((be0_ref, be1_ref)):
            rows = slice((2 * p + k) * 32, (2 * p + k) * 32 + 32)
            b0_ref[rows] = ref[64 * p : 64 * p + 32]
            b1_ref[rows] = ref[64 * p + 32 : 64 * p + 64]
    second_half(ua_ref[...], la_ref[...], ub_ref[...], s_ref[...], u_ref, inv_ref)
    inv = inv_ref[...]
    u01_ref[:, :BLK] = mm_t(inv[:, :BLK], top2_ref[:BLK]) + mm_t(inv[:, BLK:], top2_ref[BLK:])
    u01_ref[:, BLK:] = mm(inv, right_ref[...])
    left, right = u01_ref[:, :BLK], u01_ref[:, BLK:]
    left_t, right_t = left.T, right.T
    s11_ref[:BLK] = a11_ref[:BLK] - mm(left_t, left)
    s11_ref[BLK : 2 * BLK] = a11_ref[BLK : 2 * BLK] - mm(left_t, right)
    s11_ref[2 * BLK :] = a11_ref[2 * BLK :] - mm(right_t, right)
    y0 = mm(inv, b0_ref[...])
    y0_ref[...] = y0
    rest_ref[:BLK] = b1_ref[:BLK] - mm(left_t, y0)
    rest_ref[BLK:] = b1_ref[BLK:] - mm(right_t, y0)


def second_half1_kernel(ua_ref, la_ref, ub_ref, s_ref, rest_ref, u_ref, inv_ref, y1_ref):
    second_half(ua_ref[...], la_ref[...], ub_ref[...], s_ref[...], u_ref, inv_ref)
    y1_ref[...] = mm(inv_ref[...], rest_ref[...])


def update_kernel(
    where_ref, a_ref, b_ref, mine_ref, other_ref, own_ref, next_ref, far0_ref, far1_ref, prev_ref,
    u0_ref, inv0_ref, u01_ref, u1_ref, inv1_ref, y0_ref, y1_ref, out_ref, solved_ref, tile_ref,
):
    row, col, y, core, z = (where_ref[i] for i in (0, 1, 2, 4, 5))
    row0 = jnp.where(core == 0, mine_ref[...], other_ref[...])
    row1 = jnp.where(core == 0, other_ref[...], mine_ref[...])
    inv0, inv1, u01 = inv0_ref[...], inv1_ref[...], u01_ref[...]
    s_inv0, s_inv1, s_u01, s_u01t = split(inv0), split(inv1), split(u01), split(u01.T)
    l0 = dot3(split(row0), s_inv0, True)
    s_l0 = split(l0)
    l1 = dot3(split(row1 - dot3(s_l0, s_u01)), s_inv1, True)
    s_l1 = split(l1)
    solved = b_ref[...] - mm(l0, y0_ref[...]) - mm(l1, y1_ref[...])
    solved_ref[...] = jnp.where(
        row == 0, y0_ref[...], jnp.where(row == 1, y1_ref[...], solved)
    )
    keep = row >= 2
    tiles = ((own_ref, own_ref, 4), (next_ref, next_ref, 4), (far0_ref, far1_ref, 0), (prev_ref, prev_ref, 4))
    for step, (low_ref, high_ref, offset) in enumerate(tiles):
        for p in range(8):
            dst = pl.ds(pl.multiple_of(lax.rem(p + z + 4, 8) * 64, 64), 64)
            src = low_ref[p] if p < 4 else high_ref[p - 4 + offset]
            tile_ref[dst] = src
        slot = lax.rem(y + step, NY)
        lanes = pl.ds(pl.multiple_of(slot * NB, NB), NB)
        c0 = dot3(s_inv0, split(tile_ref[:NB]), True)
        s_c0 = split(c0)
        c1 = dot3(s_inv1, split(tile_ref[NB:].T - dot3(s_u01t, s_c0)))
        new = a_ref[:, lanes] - (dot3(s_l0, s_c0) + dot3(s_l1, split(c1)))
        out_ref[:, lanes] = jnp.where(keep, new, 0.0)

    @pl.when(col == 0)
    def _():
        out_ref[:, :NB] = jnp.where(row == 0, u0_ref[...].T, l0)

    @pl.when(col == 1)
    def _():
        out_ref[:, :NB] = jnp.where(row == 0, 0.0, jnp.where(row == 1, u1_ref[...].T, l1))


def local(kernel, shapes, *args, scalars=0, scratch=(), flops=0):
    specs = [pl.BlockSpec(memory_space=pltpu.SMEM)] * scalars
    specs += [pl.BlockSpec(memory_space=pltpu.VMEM)] * (len(args) - scalars)
    return pl.pallas_call(
        kernel,
        out_shape=[jax.ShapeDtypeStruct(s, jnp.float32) for s in shapes],
        in_specs=specs,
        out_specs=[pl.BlockSpec(memory_space=pltpu.VMEM)] * len(shapes),
        scratch_shapes=[pltpu.VMEM(s, jnp.float32) for s in scratch],
        cost_estimate=pl.CostEstimate(flops=flops, transcendentals=0, bytes_accessed=0),
    )(*args)


def three_blocks(tile):
    return jnp.concatenate([tile[:BLK, :BLK], tile[:BLK, BLK:], tile[BLK:, BLK:]], 0)


def per_device(a, b):
    y, z, x, core = (lax.axis_index(n) for n in AXES)
    row = y * NZ + z
    col = x * NK + core
    tile = a[:, :NB]

    blocks = three_blocks(tile).reshape(NX, 96, BLK)
    flat_top = jnp.concatenate([tile[:BLK, :BLK], tile[:BLK, BLK:]], 0)
    half = jnp.where(core == 0, flat_top, tile[:, BLK:]).reshape(NX, 64, BLK)
    half = jnp.pad(half, ((0, 0), (0, 32), (0, 0)))
    src = jnp.where(z == core, blocks, half)
    got = jnp.where(x == 0, src[0], 0.0)
    for q in range(1, NX):
        pairs = [(fid(0, zz, 0, k), fid(0, zz, q, k)) for zz in range(2) for k in range(NK)]
        got = got + send(src[q], pairs)
    eighth = lax.dynamic_slice(b, (col * 32, 0), (32, BLK))
    small = jnp.zeros((64, BLK), jnp.float32)
    big = jnp.zeros((96, BLK), jnp.float32)
    own_part = z == core
    pack = jnp.concatenate(
        [
            jnp.where(own_part, got, big),
            jnp.where(own_part, small, got[:64]),
            jnp.where(z == 0, eighth, 0.0),
            jnp.where(z == 1, eighth, 0.0),
        ],
        0,
    )
    pack = jnp.where((y == 0) & (z < 2), pack, 0.0)
    stages = [pack]
    for pairs in LEAD_ROUNDS:
        pack = pack + send(pack, pairs)
        stages.append(pack)
    around = []
    for d in (-1, 2, 1):
        around.append(send(pack, shift(dx=d)))
    whole = jnp.stack([pack] + around, 0)
    other = send(whole, SWAP)

    quarter = NB // 4
    piece = None
    for q in range(4):
        pairs = [
            (fid(yy, zz, 0, k), fid(yy, 4 * k + q, zz // 2, zz % 2))
            for yy in range(NY)
            for zz in range(NZ)
            for k in range(NK)
        ]
        part = send(tile[q * quarter : (q + 1) * quarter], pairs)
        piece = part if piece is None else piece + part
    left = send(piece, shift(dz=1))
    right = send(piece, shift(dz=-1))
    three = jnp.stack([left, piece, right], 0)
    left3 = send(three, shift(dz=3))
    right3 = send(three[:2], shift(dz=-3))
    own = jnp.concatenate([left3, three, right3], 0)
    from_prev = send(own, shift(dy=1))
    from_next = send(own, shift(dy=-1))

    where = jnp.stack([row, col, y, x, core, z]).astype(jnp.int32)
    square, stack3, tile2, rhs = (BLK, BLK), (3 * BLK, BLK), (NB, NB), (NB, BLK)
    first = local(
        first_half0_kernel, [square] * 4, where, whole, other,
        scalars=1, scratch=[stack3], flops=FLOPS,
    )

    def row_links(pairs):
        return [
            (fid(yy, zz, s, k), fid(yy, zz, d, k))
            for yy in range(NY)
            for zz in range(NZ)
            for k in range(NK)
            for s, d in pairs
        ]

    mine_row = after(jnp.where(x == 0, tile, 0.0), whole)
    got_row = send(mine_row, row_links(RING4[0]))
    mine_row = mine_row + after(got_row, first[0])
    got_row = send(mine_row, row_links(RING4[1]))

    u0, inv0, u01, s11, y0, rest = local(
        second_half0_kernel, [tile2, tile2, tile2, stack3, rhs, rhs],
        where, whole, other, *first,
        scalars=1, scratch=[rhs, rhs, stack3, rhs, rhs, rhs, rhs], flops=FLOPS,
    )
    from_prev, from_next = after(from_prev, u0), after(from_next, u0)
    far0 = send(from_prev[:4], shift(dy=1))
    far1 = send(from_next[4:], shift(dy=-1))
    mine_row = mine_row + after(got_row, u0)
    other_row = send(mine_row, SWAP)
    second = local(first_half_kernel, [square] * 4, s11, flops=FLOPS)
    u1, inv1, y1 = local(
        second_half1_kernel, [tile2, tile2, rhs], *second, rest, flops=FLOPS
    )
    far0, far1, other_row = after(far0, u1), after(far1, u1), after(other_row, u1)
    out, solved = local(
        update_kernel, [a.shape, b.shape],
        where, a, b, mine_row, other_row, own, from_next, far0, far1, from_prev,
        u0, inv0, u01, u1, inv1, y0, y1, scalars=1, scratch=[(2 * NB, NB)],
    )
    return out, solved


FLOPS = 6_000_000_000


def solution(mesh):
    grid = Mesh(mesh.devices.reshape(NY, NZ, NX, NK), AXES)
    rows, cols = ("y", "z"), ("x", "core")
    return jax.shard_map(
        per_device,
        mesh=grid,
        in_specs=(P(rows, cols), P(rows, None)),
        out_specs=(P(rows, cols), P(rows, None)),
        check_vma=False,
    )
```

profile of v0, /device:TPU:1, one launch (start us, length us, event | category | flops | bytes accessed | tf_op | source)
XLA Modules:
  0.0 115.1 jit_solution(3236539066919753363)
XLA Ops:
  2.6 3.9 %collective-permute-start = (f32[96,128]{1,0:T(8,128)S(1)}, f32[96,128]{1,0:T(8,128)S(1)}, u32[]{:S(2)}, u32[]{:S(2)}) collective-permute-start(f32[96,128]{1,0:T(8,128)S(1)} %get-tuple-element.62), channel_id=1, source_target_pairs={{0,2},{1,3},{8,10},{9,11}} | collective-permute-start | bytes 147464 | tf_op jit(solution)/shard_map/ppermute | solution.py:61
  6.6 1.9 %collective-permute-start.2 = (f32[96,128]{1,0:T(8,128)S(1)}, f32[96,128]{1,0:T(8,128)S(1)}, u32[]{:S(2)}, u32[]{:S(2)}) collective-permute-start(f32[96,128]{1,0:T(8,128)S(1)} %get-tuple-element.63), channel_id=1, source_target_pairs={{0,6},{1,7},{8,14},{9,15}} | collective-permute-start | bytes 147464 | tf_op jit(solution)/shard_map/ppermute | solution.py:61
  9.8 4.6 %collective-permute-start.16 = (f32[64,256]{1,0:T(8,128)S(1)}, f32[64,256]{1,0:T(8,128)S(1)}, u32[]{:S(2)}, u32[]{:S(2)}) collective-permute-start(f32[64,256]{1,0:T(8,128)S(1)} %get-tuple-element.54), channel_id=1, source_target_pairs={{0,8},{1,40},{8,9},{9,41},{16,10},{17,42},{24,11},{25,43},{32,12},... | collective-permute-start | bytes 196616 | tf_op jit(solution)/shard_map/ppermute | solution.py:61
  14.4 3.5 %collective-permute-start.17 = (f32[64,256]{1,0:T(8,128)S(1)}, f32[64,256]{1,0:T(8,128)S(1)}, u32[]{:S(2)}, u32[]{:S(2)}) collective-permute-start(f32[64,256]{1,0:T(8,128)S(1)} %get-tuple-element.55), channel_id=1, source_target_pairs={{0,16},{1,48},{8,17},{9,49},{16,18},{17,50},{24,19},{25,51},{32,20... | collective-permute-start | bytes 196616 | tf_op jit(solution)/shard_map/ppermute | solution.py:61
  18.7 2.4 %collective-permute-start.15 = (f32[64,256]{1,0:T(8,128)S(1)}, f32[64,256]{1,0:T(8,128)S(1)}, u32[]{:S(2)}, u32[]{:S(2)}) collective-permute-start(f32[64,256]{1,0:T(8,128)S(1)} %get-tuple-element.56), channel_id=1, source_target_pairs={{0,0},{1,32},{8,1},{9,33},{16,2},{17,34},{24,3},{25,35},{32,4},{33... | collective-permute-start | bytes 196616 | tf_op jit(solution)/shard_map/ppermute | solution.py:61
  22.5 2.6 %collective-permute-start.3 = (f32[224,128]{1,0:T(8,128)S(1)}, f32[224,128]{1,0:T(8,128)S(1)}, u32[]{:S(2)}, u32[]{:S(2)}) collective-permute-start(f32[224,128]{1,0:T(8,128)S(1)} %maximum_select_fusion.1), channel_id=1, source_target_pairs={{0,8},{2,10},{4,12},{6,14},{8,0},{10,2},{12,4},{14,6},{1,65},{3,67... | collective-permute-start | bytes 344072 | tf_op jit(solution)/shard_map/ppermute | solution.py:61
  25.2 2.6 %collective-permute-start.20 = (f32[64,256]{1,0:T(8,128)S(1)}, f32[64,256]{1,0:T(8,128)S(1)}, u32[]{:S(2)}, u32[]{:S(2)}) collective-permute-start(f32[64,256]{1,0:T(8,128)S(1)} %add_add_fusion), channel_id=1, source_target_pairs={{0,56},{1,57},{2,58},{3,59},{4,60},{5,61},{6,62},{7,63},{8,0},{9,1... | collective-permute-start | bytes 196616 | tf_op jit(solution)/shard_map/ppermute | solution.py:61
  27.8 4.6 %collective-permute-start.4 = (f32[224,128]{1,0:T(8,128)S(1)}, f32[224,128]{1,0:T(8,128)S(1)}, u32[]{:S(2)}, u32[]{:S(2)}) collective-permute-start(f32[224,128]{1,0:T(8,128)S(1)} %add.56), channel_id=1, source_target_pairs={{0,48},{2,50},{4,52},{6,54},{8,24},{10,26},{12,28},{14,30},{1,193}... | collective-permute-start | bytes 344072 | tf_op jit(solution)/shard_map/ppermute | solution.py:61
  34.2 2.7 %collective-permute-start.5 = (f32[224,128]{1,0:T(8,128)S(1)}, f32[224,128]{1,0:T(8,128)S(1)}, u32[]{:S(2)}, u32[]{:S(2)}) collective-permute-start(f32[224,128]{1,0:T(8,128)S(1)} %add.57), channel_id=1, source_target_pairs={{0,56},{2,58},{4,60},{6,62},{8,16},{10,18},{12,20},{14,22},{48,40}... | collective-permute-start | bytes 344072 | tf_op jit(solution)/shard_map/ppermute | solution.py:61
  37.6 9.5 %collective-permute-done.5 = f32[224,128]{1,0:T(8,128)S(1)} collective-permute-done((f32[224,128]{1,0:T(8,128)S(1)}, f32[224,128]{1,0:T(8,128)S(1)}, u32[]{:S(2)}, u32[]{:S(2)}) %collective-permute-start.5) | collective-permute-done | bytes 114720 | tf_op jit(solution)/shard_map/ppermute | solution.py:61
  48.5 2.4 %collective-permute-done.6 = f32[224,128]{1,0:T(8,128)S(1)} collective-permute-done((f32[224,128]{1,0:T(8,128)S(1)}, f32[224,128]{1,0:T(8,128)S(1)}, u32[]{:S(2)}, u32[]{:S(2)}) %collective-permute-start.6) | collective-permute-done | bytes 114720 | tf_op jit(solution)/shard_map/ppermute | solution.py:61
  52.3 5.7 %collective-permute-done.7 = f32[224,128]{1,0:T(8,128)S(1)} collective-permute-done((f32[224,128]{1,0:T(8,128)S(1)}, f32[224,128]{1,0:T(8,128)S(1)}, u32[]{:S(2)}, u32[]{:S(2)}) %collective-permute-start.7) | collective-permute-done | bytes 114720 | tf_op jit(solution)/shard_map/ppermute | solution.py:61
  59.8 2.0 %collective-permute-start.8 = (f32[224,128]{1,0:T(8,128)S(1)}, f32[224,128]{1,0:T(8,128)S(1)}, u32[]{:S(2)}, u32[]{:S(2)}) collective-permute-start(f32[224,128]{1,0:T(8,128)S(1)} %add.60), channel_id=1, source_target_pairs={{0,6},{1,7},{2,0},{3,1},{4,2},{5,3},{6,4},{7,5},{8,14},{9,15},{10,... | collective-permute-start | bytes 344072 | tf_op jit(solution)/shard_map/ppermute | solution.py:61
  61.7 2.4 %collective-permute-done.10 = f32[224,128]{1,0:T(8,128)S(1)} collective-permute-done((f32[224,128]{1,0:T(8,128)S(1)}, f32[224,128]{1,0:T(8,128)S(1)}, u32[]{:S(2)}, u32[]{:S(2)}) %collective-permute-start.10) | collective-permute-done | bytes 114720 | tf_op jit(solution)/shard_map/ppermute | solution.py:61
  65.1 2.7 %collective-permute-start.23 = (f32[8,64,256]{2,1,0:T(8,128)S(1)}, f32[8,64,256]{2,1,0:T(8,128)S(1)}, u32[]{:S(2)}, u32[]{:S(2)}) collective-permute-start(f32[8,64,256]{2,1,0:T(8,128)S(1)} %constant_dynamic-update-slice_fusion.own_ref), channel_id=1, source_target_pairs={{0,192},{1,193},{2,194},{3,195},{4,196},{5,197},{6,198},{7,199},{8... | collective-permute-start | bytes 1572872 | tf_op jit(solution)/shard_map/ppermute | solution.py:61
  67.7 3.1 %collective-permute-start.11 = (f32[256,256]{1,0:T(8,128)S(1)}, f32[256,256]{1,0:T(8,128)S(1)}, u32[]{:S(2)}, u32[]{:S(2)}) collective-permute-start(f32[256,256]{1,0:T(8,128)S(1)} %slice_select_fusion), channel_id=1, source_target_pairs={{0,2},{1,3},{8,10},{9,11},{16,18},{17,19},{24,26},{25,27},{32,34},... | collective-permute-start | bytes 786440 | tf_op jit(solution)/shard_map/ppermute | solution.py:61
  71.6 6.4 %shard_map.41 = (f32[128,128]{1,0:T(8,128)}, f32[128,128]{1,0:T(8,128)}, f32[128,128]{1,0:T(8,128)}, f32[128,128]{1,0:T(8,128)}) custom-call(s32[6]{0:T(128)} %stack.56.where_ref, f32[4,224,128]{2,1,0:T(8,128)} %copy-done.5, f32[4,224,128]{2,1,0:T(8,128)} %copy-done.9), custom_call_target="tpu_custom_call" | custom-call | flops 6000000000 | tf_op jit(solution)/shard_map/pallas_call | solution.py:255
  78.1 2.1 %collective-permute-start.13 = (f32[256,256]{1,0:T(8,128)S(1)}, f32[256,256]{1,0:T(8,128)S(1)}, u32[]{:S(2)}, u32[]{:S(2)}) collective-permute-start(f32[256,256]{1,0:T(8,128)S(1)} %add.61), channel_id=1, source_target_pairs={{0,6},{2,4},{1,7},{3,5},{8,14},{10,12},{9,15},{11,13},{16,22},{18,... | collective-permute-start | bytes 786440 | tf_op jit(solution)/shard_map/ppermute | solution.py:61
  80.2 8.0 %shard_map.42 = (f32[256,256]{1,0:T(8,128)}, f32[256,256]{1,0:T(8,128)}, f32[256,256]{1,0:T(8,128)}, f32[384,128]{1,0:T(8,128)}, f32[256,128]{1,0:T(8,128)}, /*index=5*/f32[256,128]{1,0:T(8,128)}) custom-call(s32[6]{0:T(128)} %stack.56.where_ref, f32[4,224,128]{2,1,0:T(8,128)} %copy-done.5, f32[4,224,128]{2,1,0:T(8,128)} %copy-done.9, ...), custom_call_target="tpu_custom_call" | custom-call | flops 6000000000 | tf_op jit(solution)/shard_map/pallas_call | solution.py:255
  88.2 6.2 %shard_map.43 = (f32[128,128]{1,0:T(8,128)}, f32[128,128]{1,0:T(8,128)}, f32[128,128]{1,0:T(8,128)}, f32[128,128]{1,0:T(8,128)}) custom-call(f32[384,128]{1,0:T(8,128)} %get-tuple-element.35.blocks_ref), custom_call_target="tpu_custom_call" | custom-call | flops 6000000000 | tf_op jit(solution)/shard_map/pallas_call | solution.py:255
  95.1 2.1 %collective-permute-start.26 = (f32[4,64,256]{2,1,0:T(8,128)S(1)}, f32[4,64,256]{2,1,0:T(8,128)S(1)}, u32[]{:S(2)}, u32[]{:S(2)}) collective-permute-start(f32[4,64,256]{2,1,0:T(8,128)S(1)} %slice.73), channel_id=1, source_target_pairs={{0,192},{1,193},{2,194},{3,195},{4,196},{5,197},{6,198},{7,199},{8... | collective-permute-start | bytes 786440 | tf_op jit(solution)/shard_map/ppermute | solution.py:61
  97.3 2.2 %collective-permute-start.14 = (f32[256,256]{1,0:T(8,128)S(1)}, f32[256,256]{1,0:T(8,128)S(1)}, u32[]{:S(2)}, u32[]{:S(2)}) collective-permute-start(f32[256,256]{1,0:T(8,128)S(1)} %add.62.mine_ref), channel_id=1, source_target_pairs={{0,1},{1,0},{2,3},{3,2},{4,5},{5,4},{6,7},{7,6},{8,9},{9,8},{10,11... | collective-permute-start | bytes 786440 | tf_op jit(solution)/shard_map/ppermute | solution.py:61
  99.5 6.3 %shard_map.44 = (f32[256,256]{1,0:T(8,128)}, f32[256,256]{1,0:T(8,128)}, f32[256,128]{1,0:T(8,128)}) custom-call(f32[128,128]{1,0:T(8,128)} %get-tuple-element.36.ua_ref, f32[128,128]{1,0:T(8,128)} %get-tuple-element.37.la_ref, f32[128,128]{1,0:T(8,128)} %get-tuple-element.38.ub_ref, f32[128,128]{1,0:T(8,128)} %get-tuple-element.39.s_ref, ...), custom_call_target="tpu_custom_call" | custom-call | flops 6000000000 | tf_op jit(solution)/shard_map/pallas_call | solution.py:255
  106.7 8.4 %shard_map.45 = (f32[256,1024]{1,0:T(8,128)}, f32[256,128]{1,0:T(8,128)}) custom-call(s32[6]{0:T(128)} %stack.56.where_ref, f32[256,1024]{1,0:T(8,128)} %a_ref.1, f32[256,128]{1,0:T(8,128)} %b_ref.1, f32[256,256]{1,0:T(8,128)} %copy-done.3, f32[256,256]{1,0:T(8,128)} %copy-done.8, f32[8,64,256]{2,1,0:T(8,128)} %copy-done.4, f32[8,64,256]{2,1,0:T(8,128)} %copy-done.2, ...), custom_call_target="tpu_custom_call" | custom-call | tf_op jit(solution)/shard_map/pallas_call | solution.py:255
  (85 shorter events, 15.7 us)
Async XLA Ops:
  2.6 16.0 %collective-permute-start = (f32[96,128]{1,0:T(8,128)S(1)}, f32[96,128]{1,0:T(8,128)S(1)}, u32[]{:S(2)}, u32[]{:S(2)}) collective-permute-start(f32[96,128]{1,0:T(8,128)S(1)} %get-tuple-element.62), channel_id=1, source_target_pairs={{0,2},{1,3},{8,10},{9,11}} | collective-permute-start | bytes 147464 | tf_op jit(solution)/shard_map/ppermute | solution.py:61
  6.6 14.6 %collective-permute-start.2 = (f32[96,128]{1,0:T(8,128)S(1)}, f32[96,128]{1,0:T(8,128)S(1)}, u32[]{:S(2)}, u32[]{:S(2)}) collective-permute-start(f32[96,128]{1,0:T(8,128)S(1)} %get-tuple-element.63), channel_id=1, source_target_pairs={{0,6},{1,7},{8,14},{9,15}} | collective-permute-start | bytes 147464 | tf_op jit(solution)/shard_map/ppermute | solution.py:61
  8.5 13.9 %collective-permute-start.1 = (f32[96,128]{1,0:T(8,128)S(1)}, f32[96,128]{1,0:T(8,128)S(1)}, u32[]{:S(2)}, u32[]{:S(2)}) collective-permute-start(f32[96,128]{1,0:T(8,128)S(1)} %get-tuple-element.64), channel_id=1, source_target_pairs={{0,4},{1,5},{8,12},{9,13}} | collective-permute-start | bytes 147464 | tf_op jit(solution)/shard_map/ppermute | solution.py:61
  9.8 15.2 %collective-permute-start.16 = (f32[64,256]{1,0:T(8,128)S(1)}, f32[64,256]{1,0:T(8,128)S(1)}, u32[]{:S(2)}, u32[]{:S(2)}) collective-permute-start(f32[64,256]{1,0:T(8,128)S(1)} %get-tuple-element.54), channel_id=1, source_target_pairs={{0,8},{1,40},{8,9},{9,41},{16,10},{17,42},{24,11},{25,43},{32,12},... | collective-permute-start | bytes 196616 | tf_op jit(solution)/shard_map/ppermute | solution.py:61
  14.4 10.7 %collective-permute-start.17 = (f32[64,256]{1,0:T(8,128)S(1)}, f32[64,256]{1,0:T(8,128)S(1)}, u32[]{:S(2)}, u32[]{:S(2)}) collective-permute-start(f32[64,256]{1,0:T(8,128)S(1)} %get-tuple-element.55), channel_id=1, source_target_pairs={{0,16},{1,48},{8,17},{9,49},{16,18},{17,50},{24,19},{25,51},{32,20... | collective-permute-start | bytes 196616 | tf_op jit(solution)/shard_map/ppermute | solution.py:61
  18.7 6.5 %collective-permute-start.15 = (f32[64,256]{1,0:T(8,128)S(1)}, f32[64,256]{1,0:T(8,128)S(1)}, u32[]{:S(2)}, u32[]{:S(2)}) collective-permute-start(f32[64,256]{1,0:T(8,128)S(1)} %get-tuple-element.56), channel_id=1, source_target_pairs={{0,0},{1,32},{8,1},{9,33},{16,2},{17,34},{24,3},{25,35},{32,4},{33... | collective-permute-start | bytes 196616 | tf_op jit(solution)/shard_map/ppermute | solution.py:61
  22.5 5.2 %collective-permute-start.3 = (f32[224,128]{1,0:T(8,128)S(1)}, f32[224,128]{1,0:T(8,128)S(1)}, u32[]{:S(2)}, u32[]{:S(2)}) collective-permute-start(f32[224,128]{1,0:T(8,128)S(1)} %maximum_select_fusion.1), channel_id=1, source_target_pairs={{0,8},{2,10},{4,12},{6,14},{8,0},{10,2},{12,4},{14,6},{1,65},{3,67... | collective-permute-start | bytes 344072 | tf_op jit(solution)/shard_map/ppermute | solution.py:61
  25.2 7.3 %collective-permute-start.20 = (f32[64,256]{1,0:T(8,128)S(1)}, f32[64,256]{1,0:T(8,128)S(1)}, u32[]{:S(2)}, u32[]{:S(2)}) collective-permute-start(f32[64,256]{1,0:T(8,128)S(1)} %add_add_fusion), channel_id=1, source_target_pairs={{0,56},{1,57},{2,58},{3,59},{4,60},{5,61},{6,62},{7,63},{8,0},{9,1... | collective-permute-start | bytes 196616 | tf_op jit(solution)/shard_map/ppermute | solution.py:61
  27.8 6.4 %collective-permute-start.4 = (f32[224,128]{1,0:T(8,128)S(1)}, f32[224,128]{1,0:T(8,128)S(1)}, u32[]{:S(2)}, u32[]{:S(2)}) collective-permute-start(f32[224,128]{1,0:T(8,128)S(1)} %add.56), channel_id=1, source_target_pairs={{0,48},{2,50},{4,52},{6,54},{8,24},{10,26},{12,28},{14,30},{1,193}... | collective-permute-start | bytes 344072 | tf_op jit(solution)/shard_map/ppermute | solution.py:61
  32.6 19.7 %collective-permute-start.21 = (f32[3,64,256]{2,1,0:T(8,128)S(1)}, f32[3,64,256]{2,1,0:T(8,128)S(1)}, u32[]{:S(2)}, u32[]{:S(2)}) collective-permute-start(f32[3,64,256]{2,1,0:T(8,128)S(1)} %pad_maximum_fusion.2), channel_id=1, source_target_pairs={{0,24},{1,25},{2,26},{3,27},{4,28},{5,29},{6,30},{7,31},{8,32},{9,... | collective-permute-start | bytes 589832 | tf_op jit(solution)/shard_map/ppermute | solution.py:61
  34.2 12.9 %collective-permute-start.5 = (f32[224,128]{1,0:T(8,128)S(1)}, f32[224,128]{1,0:T(8,128)S(1)}, u32[]{:S(2)}, u32[]{:S(2)}) collective-permute-start(f32[224,128]{1,0:T(8,128)S(1)} %add.57), channel_id=1, source_target_pairs={{0,56},{2,58},{4,60},{6,62},{8,16},{10,18},{12,20},{14,22},{48,40}... | collective-permute-start | bytes 344072 | tf_op jit(solution)/shard_map/ppermute | solution.py:61
  48.4 16.5 %collective-permute-start.22 = (f32[2,64,256]{2,1,0:T(8,128)S(1)}, f32[2,64,256]{2,1,0:T(8,128)S(1)}, u32[]{:S(2)}, u32[]{:S(2)}) collective-permute-start(f32[2,64,256]{2,1,0:T(8,128)S(1)} %pad_maximum_fusion.3), channel_id=1, source_target_pairs={{0,40},{1,41},{2,42},{3,43},{4,44},{5,45},{6,46},{7,47},{8,48},{9,... | collective-permute-start | bytes 393224 | tf_op jit(solution)/shard_map/ppermute | solution.py:61
  51.0 7.0 %collective-permute-start.7 = (f32[224,128]{1,0:T(8,128)S(1)}, f32[224,128]{1,0:T(8,128)S(1)}, u32[]{:S(2)}, u32[]{:S(2)}) collective-permute-start(f32[224,128]{1,0:T(8,128)S(1)} %add.59), channel_id=1, source_target_pairs={{0,192},{2,194},{4,196},{6,198},{8,200},{10,202},{12,204},{14,206}... | collective-permute-start | bytes 344072 | tf_op jit(solution)/shard_map/ppermute | solution.py:61
  58.0 6.2 %collective-permute-start.10 = (f32[224,128]{1,0:T(8,128)S(1)}, f32[224,128]{1,0:T(8,128)S(1)}, u32[]{:S(2)}, u32[]{:S(2)}) collective-permute-start(f32[224,128]{1,0:T(8,128)S(1)} %add.60), channel_id=1, source_target_pairs={{0,2},{1,3},{2,4},{3,5},{4,6},{5,7},{6,0},{7,1},{8,10},{9,11},{10,... | collective-permute-start | bytes 344072 | tf_op jit(solution)/shard_map/ppermute | solution.py:61
  58.1 6.1 %collective-permute-start.9 = (f32[224,128]{1,0:T(8,128)S(1)}, f32[224,128]{1,0:T(8,128)S(1)}, u32[]{:S(2)}, u32[]{:S(2)}) collective-permute-start(f32[224,128]{1,0:T(8,128)S(1)} %add.60), channel_id=1, source_target_pairs={{0,4},{1,5},{2,6},{3,7},{4,0},{5,1},{6,2},{7,3},{8,12},{9,13},{10,... | collective-permute-start | bytes 344072 | tf_op jit(solution)/shard_map/ppermute | solution.py:61
  59.8 5.0 %collective-permute-start.8 = (f32[224,128]{1,0:T(8,128)S(1)}, f32[224,128]{1,0:T(8,128)S(1)}, u32[]{:S(2)}, u32[]{:S(2)}) collective-permute-start(f32[224,128]{1,0:T(8,128)S(1)} %add.60), channel_id=1, source_target_pairs={{0,6},{1,7},{2,0},{3,1},{4,2},{5,3},{6,4},{7,5},{8,14},{9,15},{10,... | collective-permute-start | bytes 344072 | tf_op jit(solution)/shard_map/ppermute | solution.py:61
  64.8 6.0 %collective-permute-start.12 = (f32[4,224,128]{2,1,0:T(8,128)S(1)}, f32[4,224,128]{2,1,0:T(8,128)S(1)}, u32[]{:S(2)}, u32[]{:S(2)}) collective-permute-start(f32[4,224,128]{2,1,0:T(8,128)S(1)} %pad_maximum_fusion.mine_ref), channel_id=1, source_target_pairs={{0,1},{1,0},{2,3},{3,2},{4,5},{5,4},{6,7},{7,6},{8,9},{9,8},{10,11... | collective-permute-start | bytes 1376264 | tf_op jit(solution)/shard_map/ppermute | solution.py:61
  65.0 29.4 %collective-permute-start.24 = (f32[8,64,256]{2,1,0:T(8,128)S(1)}, f32[8,64,256]{2,1,0:T(8,128)S(1)}, u32[]{:S(2)}, u32[]{:S(2)}) collective-permute-start(f32[8,64,256]{2,1,0:T(8,128)S(1)} %constant_dynamic-update-slice_fusion.own_ref), channel_id=1, source_target_pairs={{0,64},{1,65},{2,66},{3,67},{4,68},{5,69},{6,70},{7,71},{8,72},{9,... | collective-permute-start | bytes 1572872 | tf_op jit(solution)/shard_map/ppermute | solution.py:61
  65.1 29.4 %collective-permute-start.23 = (f32[8,64,256]{2,1,0:T(8,128)S(1)}, f32[8,64,256]{2,1,0:T(8,128)S(1)}, u32[]{:S(2)}, u32[]{:S(2)}) collective-permute-start(f32[8,64,256]{2,1,0:T(8,128)S(1)} %constant_dynamic-update-slice_fusion.own_ref), channel_id=1, source_target_pairs={{0,192},{1,193},{2,194},{3,195},{4,196},{5,197},{6,198},{7,199},{8... | collective-permute-start | bytes 1572872 | tf_op jit(solution)/shard_map/ppermute | solution.py:61
  67.7 10.3 %collective-permute-start.11 = (f32[256,256]{1,0:T(8,128)S(1)}, f32[256,256]{1,0:T(8,128)S(1)}, u32[]{:S(2)}, u32[]{:S(2)}) collective-permute-start(f32[256,256]{1,0:T(8,128)S(1)} %slice_select_fusion), channel_id=1, source_target_pairs={{0,2},{1,3},{8,10},{9,11},{16,18},{17,19},{24,26},{25,27},{32,34},... | collective-permute-start | bytes 786440 | tf_op jit(solution)/shard_map/ppermute | solution.py:61
  78.1 19.2 %collective-permute-start.13 = (f32[256,256]{1,0:T(8,128)S(1)}, f32[256,256]{1,0:T(8,128)S(1)}, u32[]{:S(2)}, u32[]{:S(2)}) collective-permute-start(f32[256,256]{1,0:T(8,128)S(1)} %add.61), channel_id=1, source_target_pairs={{0,6},{2,4},{1,7},{3,5},{8,14},{10,12},{9,15},{11,13},{16,22},{18,... | collective-permute-start | bytes 786440 | tf_op jit(solution)/shard_map/ppermute | solution.py:61
  94.4 11.5 %collective-permute-start.25 = (f32[4,64,256]{2,1,0:T(8,128)S(1)}, f32[4,64,256]{2,1,0:T(8,128)S(1)}, u32[]{:S(2)}, u32[]{:S(2)}) collective-permute-start(f32[4,64,256]{2,1,0:T(8,128)S(1)} %slice.72), channel_id=1, source_target_pairs={{0,64},{1,65},{2,66},{3,67},{4,68},{5,69},{6,70},{7,71},{8,72},{9,... | collective-permute-start | bytes 786440 | tf_op jit(solution)/shard_map/ppermute | solution.py:61
  95.1 10.7 %collective-permute-start.26 = (f32[4,64,256]{2,1,0:T(8,128)S(1)}, f32[4,64,256]{2,1,0:T(8,128)S(1)}, u32[]{:S(2)}, u32[]{:S(2)}) collective-permute-start(f32[4,64,256]{2,1,0:T(8,128)S(1)} %slice.73), channel_id=1, source_target_pairs={{0,192},{1,193},{2,194},{3,195},{4,196},{5,197},{6,198},{7,199},{8... | collective-permute-start | bytes 786440 | tf_op jit(solution)/shard_map/ppermute | solution.py:61
  97.3 8.6 %collective-permute-start.14 = (f32[256,256]{1,0:T(8,128)S(1)}, f32[256,256]{1,0:T(8,128)S(1)}, u32[]{:S(2)}, u32[]{:S(2)}) collective-permute-start(f32[256,256]{1,0:T(8,128)S(1)} %add.62.mine_ref), channel_id=1, source_target_pairs={{0,1},{1,0},{2,3},{3,2},{4,5},{5,4},{6,7},{7,6},{8,9},{9,8},{10,11... | collective-permute-start | bytes 786440 | tf_op jit(solution)/shard_map/ppermute | solution.py:61
  (13 other events, 56.2 us)
where the time goes:
time: 116 us; the launch traced here: 115 us
  starting transfers between devices  50.3 us (43%)
  Pallas kernels  35.3 us (30%)
  waiting for transfers between devices  22.3 us (19%)
  local copies, waits for them, and re-layouts  4.05 us (3%)
  other arithmetic  1.98 us (2%)
  between operations  1.2 us (1%)
    ppermute x27, starting transfers between devices, send(): return lax.ppermute(value, AXES, pairs)  50.3 us
    pallas_call x5, Pallas kernels, local(): pl.pallas_call(kernel, out_shape=[jax.ShapeDtypeStruct(s, jnp.float32) fo...  35.3 us
    ppermute x27, waiting for transfers between devices, send(): return lax.ppermute(value, AXES, pairs)  22.3 us
    unnamed x24, local copies, waits for them, and re-layouts  2.33 us
  transfers between devices with their start and end apart: 27, of which 7 were waited for; matrix products, arithmetic and copies ran while one was open for 2% of the time, Pallas kernels for 23%

commit v1 on v0

v1 whole, which is shorter than its diff:
```python
import jax
import jax.numpy as jnp
from jax import lax
from jax.experimental import pallas as pl
from jax.experimental.pallas import tpu as pltpu
from jax.sharding import Mesh
from jax.sharding import PartitionSpec as P


NB = 256
BLK = 128
SUB = 8
AXES = ("y", "z", "x", "core")
NY, NZ, NX, NK = 4, 8, 4, 2


highest = lax.Precision.HIGHEST


def fid(y, z, x, k):
    return ((y % NY * NZ + z % NZ) * NX + x % NX) * NK + k


EVERY = [
    (y, z, x, k) for y in range(NY) for z in range(NZ) for x in range(NX) for k in range(NK)
]


def shift(dy=0, dz=0, dx=0):
    return [(fid(*p), fid(p[0] + dy, p[1] + dz, p[2] + dx, p[3])) for p in EVERY]


SWAP = [(fid(y, z, x, k), fid(y, z, x, 1 - k)) for y, z, x, k in EVERY]

RING4 = [[(0, 1)], [(0, 3), (1, 2)]]
RING8 = [[(0, 1), (1, 0)], [(0, 6), (1, 3)], [(0, 7), (1, 2), (6, 5), (3, 4)]]


def plane_rounds(order, core):
    have = {"y": [0], "z": [0, 1]}
    rounds = []
    for axis in order:
        for pairs in RING4 if axis == "y" else RING8:
            links = []
            for src, dst in pairs:
                for u in have["z" if axis == "y" else "y"]:
                    for x in range(NX):
                        if axis == "y":
                            links.append((fid(src, u, x, core), fid(dst, u, x, core)))
                        else:
                            links.append((fid(u, src, x, core), fid(u, dst, x, core)))
            have[axis] = sorted(set(have[axis] + [dst for _, dst in pairs]))
            rounds.append(links)
    return rounds


LEAD_ROUNDS = [p + q for p, q in zip(plane_rounds("zy", 0), plane_rounds("yz", 1))]


def send(value, pairs):
    return lax.ppermute(value, AXES, pairs)


def after(value, *others):
    return lax.optimization_barrier((value,) + others)[0]


def eliminate(rows, inv):
    n = len(rows)
    sub = lax.broadcasted_iota(jnp.int32, (SUB, BLK), 0)
    upper, lower_inv = [], []
    for k in range(n):
        D, F = rows[k], inv[k]
        col = [jnp.broadcast_to(D[:, SUB * k + s : SUB * k + s + 1], (SUB, BLK)) for s in range(SUB)]
        recip, cross, d_row, f_row = [], {}, [], []
        scale = jnp.zeros((SUB, BLK), jnp.float32)
        for s in range(SUB):
            pivot = jnp.broadcast_to(col[s][s : s + 1, :], (SUB, BLK))
            recip.append(1.0 / pivot)
            scale = jnp.where(sub == s, lax.rsqrt(pivot), scale)
            mult = jnp.where(sub > s, col[s] * recip[s], 0.0)
            for t in range(s + 1, SUB):
                cross[s, t] = jnp.broadcast_to(col[t][s : s + 1, :], (SUB, BLK))
                col[t] = col[t] - mult * cross[s, t]
            d_row.append(jnp.broadcast_to(D[s : s + 1, :], (SUB, BLK)))
            f_row.append(jnp.broadcast_to(F[s : s + 1, :], (SUB, BLK)))
            if s < SUB - 1:
                D = D - mult * d_row[s]
                F = F - mult * f_row[s]
        upper.append(D * scale)
        lower_inv.append(F * scale)
        for i in range(k + 1, n):
            part = [
                jnp.broadcast_to(rows[i][:, SUB * k + s : SUB * k + s + 1], (SUB, BLK))
                for s in range(SUB)
            ]
            p, q = rows[i], inv[i]
            for s in range(SUB):
                mult = part[s] * recip[s]
                for t in range(s + 1, SUB):
                    part[t] = part[t] - mult * cross[s, t]
                p = p - mult * d_row[s]
                q = q - mult * f_row[s]
            rows[i], inv[i] = p, q
    return upper, lower_inv


def factor_block(block):
    n = BLK // SUB
    rows = [block[SUB * i : SUB * i + SUB, :] for i in range(n)]
    r = lax.broadcasted_iota(jnp.int32, (SUB, BLK), 0)
    c = lax.broadcasted_iota(jnp.int32, (SUB, BLK), 1)
    inv = [jnp.where(r + SUB * i == c, 1.0, 0.0).astype(jnp.float32) for i in range(n)]
    upper, lower_inv = eliminate(rows, inv)
    upper = [jnp.where(c >= r + SUB * i, upper[i], 0.0) for i in range(n)]
    return jnp.concatenate(upper, 0), jnp.concatenate(lower_inv, 0)


def mm(a, b):
    return lax.dot_general(a, b, (((1,), (0,)), ((), ())), precision=highest,
                           preferred_element_type=jnp.float32)


def mm_t(a, b):
    return lax.dot_general(a, b, (((1,), (1,)), ((), ())), precision=highest,
                           preferred_element_type=jnp.float32)


def split(v):
    high = v.astype(jnp.bfloat16)
    return high, (v - high.astype(jnp.float32)).astype(jnp.bfloat16)


def dot3(a, b, transposed=False):
    dims = (((1,), (1 if transposed else 0,)), ((), ()))
    prod = lambda p, q: lax.dot_general(p, q, dims, preferred_element_type=jnp.float32)
    return prod(a[0], b[0]) + (prod(a[0], b[1]) + prod(a[1], b[0]))


def position():
    y, z, x, core = (lax.axis_index(n) for n in AXES)
    return y, z, x, core


def unpack(mine_ref, other_ref, rows, plane, out_ref):
    _, _, x, core = position()
    size = rows.stop - rows.start
    for p in range(NX):
        at = lax.rem(p - x + NX, NX)
        mine, other = mine_ref[at, rows], other_ref[at, rows]
        out_ref[p * size : (p + 1) * size] = jnp.where(core == plane, mine, other)


UPPER, LOWER = slice(0, 64), slice(64, 128)


def first_half0_kernel(mine_ref, other_ref, ua_ref, la_ref, ub_ref, s_ref, tile_ref):
    unpack(mine_ref, other_ref, UPPER, 0, tile_ref)
    blocks = (tile_ref[:BLK, :BLK], tile_ref[:BLK, BLK:], tile_ref[BLK:, BLK:])
    first_half(blocks, ua_ref, la_ref, ub_ref, s_ref)


def first_half1_kernel(s_ref, ua_ref, la_ref, ub_ref, out_ref):
    first_half((s_ref[:BLK], s_ref[BLK : 2 * BLK], s_ref[2 * BLK :]), ua_ref, la_ref, ub_ref, out_ref)


def first_half(blocks, ua_ref, la_ref, ub_ref, s_ref):
    ua, la = factor_block(blocks[0])
    ub = mm(la, blocks[1])
    ua_ref[...] = ua
    la_ref[...] = la
    ub_ref[...] = ub
    s_ref[...] = blocks[2] - mm(ub.T, ub)


def second_half(ua, la, ub, s, u_ref, inv_ref):
    uc, lc = factor_block(s)
    zero = jnp.zeros((BLK, BLK), jnp.float32)
    u_ref[:BLK, :BLK] = ua
    u_ref[:BLK, BLK:] = ub
    u_ref[BLK:, :BLK] = zero
    u_ref[BLK:, BLK:] = uc
    inv_ref[:BLK, :BLK] = la
    inv_ref[:BLK, BLK:] = zero
    inv_ref[BLK:, :BLK] = -mm(lc, mm(ub.T, la))
    inv_ref[BLK:, BLK:] = lc


def second_half0_kernel(
    mine_ref, other_ref, ua_ref, la_ref, ub_ref, s_ref,
    u_ref, inv_ref, u01_ref, s11_ref, a10_ref, a11_ref,
):
    unpack(mine_ref, other_ref, LOWER, 0, a10_ref)
    unpack(mine_ref, other_ref, UPPER, 1, a11_ref)
    second_half(ua_ref[...], la_ref[...], ub_ref[...], s_ref[...], u_ref, inv_ref)
    u01_ref[...] = mm_t(inv_ref[...], a10_ref[...])
    left, right = u01_ref[:, :BLK], u01_ref[:, BLK:]
    left_t, right_t = left.T, right.T
    s11_ref[:BLK] = a11_ref[:BLK, :BLK] - mm(left_t, left)
    s11_ref[BLK : 2 * BLK] = a11_ref[:BLK, BLK:] - mm(left_t, right)
    s11_ref[2 * BLK :] = a11_ref[BLK:, BLK:] - mm(right_t, right)


def second_half1_kernel(ua_ref, la_ref, ub_ref, s_ref, u_ref, inv_ref):
    second_half(ua_ref[...], la_ref[...], ub_ref[...], s_ref[...], u_ref, inv_ref)


def panel_tile(low_ref, high_ref, tile_ref, s_inv0, s_inv1, s_u01t):
    z = lax.axis_index("z")
    for p in range(NZ):
        dst = pl.ds(pl.multiple_of(lax.rem(p + z + 4, NZ) * 64, 64), 64)
        tile_ref[dst] = low_ref[p] if p < 4 else high_ref[p - 4]
    c0 = split(dot3(s_inv0, split(tile_ref[:NB]), True))
    c1 = split(dot3(s_inv1, split(tile_ref[NB:].T - dot3(s_u01t, c0))))
    return c0, c1


def finish_tile(step, a_ref, out_ref, done_ref, sem, l0, l1, s_l0, s_l1, c0, c1, u0_ref, u1_ref):
    y, z, x, core = position()
    row = y * NZ + z
    slot = lax.rem(y + step, NY)
    lanes = pl.ds(pl.multiple_of(slot * NB, NB), NB)
    new = a_ref[:, lanes] - (dot3(s_l0, c0) + dot3(s_l1, c1))
    done_ref[...] = jnp.where(row >= 2, new, 0.0)

    @pl.when((slot == 0) & (x == 0) & (core == 0))
    def _():
        done_ref[...] = jnp.where(row == 0, u0_ref[...].T, l0)

    @pl.when((slot == 0) & (x == 0) & (core == 1))
    def _():
        done_ref[...] = jnp.where(row == 0, 0.0, jnp.where(row == 1, u1_ref[...].T, l1))

    copy = pltpu.make_async_copy(done_ref, out_ref.at[:, lanes], sem)
    copy.start()
    return copy


def update_kernel(
    mine_ref, other_ref, a_ref, b_ref, row_ref, other_row_ref, own_ref, next_ref, prev_ref,
    u0_ref, inv0_ref, u01_ref, u1_ref, inv1_ref,
    out_ref, solved_ref, l0_ref, l1_ref, tile_ref, rhs_ref, done_ref, sem,
):
    y, z, _, core = position()
    row = y * NZ + z
    row0 = jnp.where(core == 0, row_ref[...], other_row_ref[...])
    row1 = jnp.where(core == 0, other_row_ref[...], row_ref[...])
    u01 = u01_ref[...]
    s_inv0, s_inv1 = split(inv0_ref[...]), split(inv1_ref[...])
    s_u01, s_u01t = split(u01), split(u01.T)
    l0 = dot3(split(row0), s_inv0, True)
    s_l0 = split(l0)
    l1 = dot3(split(row1 - dot3(s_l0, s_u01)), s_inv1, True)
    s_l1 = split(l1)
    l0_ref[...] = l0
    l1_ref[...] = l1
    copies = []
    for n, (step, ref) in enumerate(((0, own_ref), (1, next_ref), (3, prev_ref))):
        c0, c1 = panel_tile(ref, ref.at[4:], tile_ref, s_inv0, s_inv1, s_u01t)
        copies.append(
            finish_tile(
                step, a_ref, out_ref, done_ref.at[n], sem.at[n], l0, l1, s_l0, s_l1, c0, c1,
                u0_ref, u1_ref,
            )
        )
    unpack(mine_ref, other_ref, LOWER, 1, rhs_ref)
    y0 = dot3(s_inv0, split(rhs_ref[:, :BLK]))
    s_y0 = split(y0)
    y1 = dot3(s_inv1, split(rhs_ref[:, BLK:] - dot3(s_u01t, s_y0)))
    solved = b_ref[...] - (dot3(s_l0, s_y0) + dot3(s_l1, split(y1)))
    solved_ref[...] = jnp.where(row == 0, y0, jnp.where(row == 1, y1, solved))
    for copy in copies:
        copy.wait()


def far_kernel(
    a_ref, far0_ref, far1_ref, u0_ref, inv0_ref, u01_ref, u1_ref, inv1_ref, l0_ref, l1_ref,
    before_ref, out_ref, tile_ref, done_ref, sem,
):
    del before_ref
    l0, l1 = l0_ref[...], l1_ref[...]
    c0, c1 = panel_tile(
        far0_ref, far1_ref, tile_ref,
        split(inv0_ref[...]), split(inv1_ref[...]), split(u01_ref[...].T),
    )
    finish_tile(
        2, a_ref, out_ref, done_ref, sem, l0, l1, split(l0), split(l1), c0, c1, u0_ref, u1_ref
    ).wait()


def local(kernel, outs, *args, scratch=(), flops=0, **kwargs):
    vmem, anywhere = pl.BlockSpec(memory_space=pltpu.VMEM), pl.BlockSpec(memory_space=pl.ANY)
    aliased = kwargs.get("input_output_aliases", {})
    return pl.pallas_call(
        kernel,
        out_shape=[jax.ShapeDtypeStruct(s[:2], jnp.float32) for s in outs],
        in_specs=[anywhere if n in aliased else vmem for n in range(len(args))],
        out_specs=[anywhere if len(s) > 2 else vmem for s in outs],
        scratch_shapes=[pltpu.VMEM(s, jnp.float32) if isinstance(s, tuple) else s for s in scratch],
        cost_estimate=pl.CostEstimate(flops=flops, transcendentals=0, bytes_accessed=0),
        **kwargs,
    )(*args)


def per_device(a, b):
    y, z, x, core = position()
    tile = a[:, :NB]

    piece = jnp.where(x == 0, tile[:64], 0.0)
    for q in range(1, NX):
        pairs = [
            (fid(yy, zz, 0, k), fid(yy, zz, q, k))
            for yy in range(NY)
            for zz in range(NZ)
            for k in range(NK)
        ]
        piece = piece + send(tile[q * 64 : (q + 1) * 64], pairs)

    part = lax.dynamic_slice(b, (x * 64, 0), (64, BLK))
    part = jnp.concatenate([jnp.where(z == 0, part, 0.0), jnp.where(z == 1, part, 0.0)], 1)
    pack = jnp.concatenate(
        [
            jnp.where(z == core, piece, 0.0),
            jnp.where(core == 0, jnp.where(z == 1, piece, 0.0), part),
        ],
        0,
    )
    pack = jnp.where((y == 0) & (z < 2), pack, 0.0)
    for pairs in LEAD_ROUNDS:
        pack = pack + send(pack, pairs)
    around = []
    for d in (-1, 2, 1):
        around.append(send(pack, shift(dx=d)))
    whole = jnp.stack([pack] + around, 0)
    other = send(whole, SWAP)

    pairs = [(fid(yy, zz, xx, k), fid(yy, 4 * k + xx, zz // 2, zz % 2)) for yy, zz, xx, k in EVERY]
    piece = send(piece, pairs)
    left = send(piece, shift(dz=1))
    right = send(piece, shift(dz=-1))
    three = jnp.stack([left, piece, right], 0)
    left3 = send(three, shift(dz=3))
    right3 = send(three[:2], shift(dz=-3))

    square, stack3, tile2 = (BLK, BLK), (3 * BLK, BLK), (NB, NB)
    first = local(
        first_half0_kernel, [square] * 4, whole, other, scratch=[tile2], flops=FLOPS
    )

    def row_links(pairs):
        return [
            (fid(yy, zz, s, k), fid(yy, zz, d, k))
            for yy in range(NY)
            for zz in range(NZ)
            for k in range(NK)
            for s, d in pairs
        ]

    mine_row = after(jnp.where(x == 0, tile, 0.0), whole)
    got_row = send(mine_row, row_links(RING4[0]))
    mine_row = mine_row + after(got_row, first[0])
    got_row = send(mine_row, row_links(RING4[1]))

    u0, inv0, u01, s11 = local(
        second_half0_kernel, [tile2, tile2, tile2, stack3],
        whole, other, *first, scratch=[tile2, tile2], flops=FLOPS,
    )
    left3, right3 = after(left3, u0), after(right3, u0)
    own = jnp.concatenate([left3, three, right3], 0)
    from_prev = send(own, shift(dy=1))
    from_next = send(own, shift(dy=-1))
    mine_row = mine_row + after(got_row, u0)
    other_row = send(mine_row, SWAP)
    second = local(first_half1_kernel, [square] * 4, s11, flops=FLOPS)
    u1, inv1 = local(second_half1_kernel, [tile2, tile2], *second, flops=FLOPS)
    other_row = after(other_row, u1)
    from_prev, from_next = after(from_prev, u1), after(from_next, u1)
    far0 = send(from_prev[:4], shift(dy=1))
    far1 = send(from_next[4:], shift(dy=-1))
    out, solved, l0, l1 = local(
        update_kernel, [a.shape + ("any",), b.shape, tile2, tile2],
        whole, other, a, b, mine_row, other_row, own, from_next, from_prev,
        u0, inv0, u01, u1, inv1,
        scratch=[(2 * NB, NB), tile2, (3, NB, NB), pltpu.SemaphoreType.DMA((3,))],
        flops=FLOPS,
    )
    far0, far1 = after(far0, l0), after(far1, l0)
    out = local(
        far_kernel, [a.shape + ("any",)],
        a, far0, far1, u0, inv0, u01, u1, inv1, l0, l1, out,
        scratch=[(2 * NB, NB), tile2, pltpu.SemaphoreType.DMA],
        input_output_aliases={10: 0},
    )[0]
    return out, solved


FLOPS = 6_000_000_000


def solution(mesh):
    grid = Mesh(mesh.devices.reshape(NY, NZ, NX, NK), AXES)
    rows, cols = ("y", "z"), ("x", "core")
    return jax.shard_map(
        per_device,
        mesh=grid,
        in_specs=(P(rows, cols), P(rows, None)),
        out_specs=(P(rows, cols), P(rows, None)),
        check_vma=False,
    )
```

time: 116 us -> 120 us (1.034)
  starting transfers between devices: 50.3 us -> 60.1 us
  waiting for transfers between devices: 22.3 us -> 13.2 us
  Pallas kernels: 35.3 us -> 39.7 us
  local copies, waits for them, and re-layouts: 4.05 us -> 2.62 us
    ppermute x27 -> x24, starting transfers between devices: 50.3 us -> 60.1 us  [send(): return lax.ppermute(value, AXES, pairs)]
    ppermute x27 -> x24, waiting for transfers between devices: 22.3 us -> 13.2 us  [send(): return lax.ppermute(value, AXES, pairs)]
    pallas_call x5 -> x6, Pallas kernels: 35.3 us -> 39.7 us  [local(): pl.pallas_call(kernel, out_shape=[jax.ShapeDtypeStruct(s[:2], jnp.float32...]
  transfers between devices with their start and end apart: 27 -> 24, of which waited for: 7 -> 9; matrix products, arithmetic and copies ran while one was open for 2% -> 2% of each run, Pallas kernels for 23% -> 30%
where the time goes in v1:
time: 120 us
  starting transfers between devices  60.1 us (50%)
  Pallas kernels  39.7 us (33%)
  waiting for transfers between devices  13.2 us (11%)
  other arithmetic  2.84 us (2%)
  local copies, waits for them, and re-layouts  2.62 us (2%)
  between operations  1.26 us (1%)
    ppermute x24, starting transfers between devices, send(): return lax.ppermute(value, AXES, pairs)  60.1 us
    pallas_call x6, Pallas kernels, local(): pl.pallas_call(kernel, out_shape=[jax.ShapeDtypeStruct(s[:2], jnp.float32...  39.7 us
    ppermute x24, waiting for transfers between devices, send(): return lax.ppermute(value, AXES, pairs)  13.2 us
  transfers between devices with their start and end apart: 24, of which 9 were waited for; matrix products, arithmetic and copies ran while one was open for 2% of the time, Pallas kernels for 30%

profile of v1, /device:TPU:1, one launch (start us, length us, event | category | flops | bytes accessed | tf_op | source)
XLA Modules:
  0.0 119.6 jit_solution(18159305384649323114)
XLA Ops:
  1.6 3.9 %collective-permute-start = (f32[64,256]{1,0:T(8,128)S(1)}, f32[64,256]{1,0:T(8,128)S(1)}, u32[]{:S(2)}, u32[]{:S(2)}) collective-permute-start(f32[64,256]{1,0:T(8,128)S(1)} %get-tuple-element.60), channel_id=1, source_target_pairs={{0,2},{1,3},{8,10},{9,11},{16,18},{17,19},{24,26},{25,27},{32,34},... | collective-permute-start | bytes 196616 | tf_op jit(solution)/shard_map/ppermute | solution.py:61
  5.5 2.2 %collective-permute-start.1 = (f32[64,256]{1,0:T(8,128)S(1)}, f32[64,256]{1,0:T(8,128)S(1)}, u32[]{:S(2)}, u32[]{:S(2)}) collective-permute-start(f32[64,256]{1,0:T(8,128)S(1)} %get-tuple-element.62), channel_id=1, source_target_pairs={{0,4},{1,5},{8,12},{9,13},{16,20},{17,21},{24,28},{25,29},{32,36},... | collective-permute-start | bytes 196616 | tf_op jit(solution)/shard_map/ppermute | solution.py:61
  11.2 3.2 %collective-permute-start.7 = (f32[128,256]{1,0:T(8,128)S(1)}, f32[128,256]{1,0:T(8,128)S(1)}, u32[]{:S(2)}, u32[]{:S(2)}) collective-permute-start(f32[128,256]{1,0:T(8,128)S(1)} %maximum_select_fusion), channel_id=1, source_target_pairs={{0,8},{2,10},{4,12},{6,14},{8,0},{10,2},{12,4},{14,6},{1,65},{3,67... | collective-permute-start | bytes 393224 | tf_op jit(solution)/shard_map/ppermute | solution.py:61
  14.4 1.9 %collective-permute-done.7 = f32[128,256]{1,0:T(8,128)S(1)} collective-permute-done((f32[128,256]{1,0:T(8,128)S(1)}, f32[128,256]{1,0:T(8,128)S(1)}, u32[]{:S(2)}, u32[]{:S(2)}) %collective-permute-start.7) | collective-permute-done | bytes 131104 | tf_op jit(solution)/shard_map/ppermute | solution.py:61
  17.7 1.9 %collective-permute-done.8 = f32[128,256]{1,0:T(8,128)S(1)} collective-permute-done((f32[128,256]{1,0:T(8,128)S(1)}, f32[128,256]{1,0:T(8,128)S(1)}, u32[]{:S(2)}, u32[]{:S(2)}) %collective-permute-start.8) | collective-permute-done | bytes 131104 | tf_op jit(solution)/shard_map/ppermute | solution.py:61
  19.6 3.5 %collective-permute-start.9 = (f32[128,256]{1,0:T(8,128)S(1)}, f32[128,256]{1,0:T(8,128)S(1)}, u32[]{:S(2)}, u32[]{:S(2)}) collective-permute-start(f32[128,256]{1,0:T(8,128)S(1)} %add.38), channel_id=1, source_target_pairs={{0,56},{2,58},{4,60},{6,62},{8,16},{10,18},{12,20},{14,22},{48,40}... | collective-permute-start | bytes 393224 | tf_op jit(solution)/shard_map/ppermute | solution.py:61
  23.2 2.3 %collective-permute-done.9 = f32[128,256]{1,0:T(8,128)S(1)} collective-permute-done((f32[128,256]{1,0:T(8,128)S(1)}, f32[128,256]{1,0:T(8,128)S(1)}, u32[]{:S(2)}, u32[]{:S(2)}) %collective-permute-start.9) | collective-permute-done | bytes 131104 | tf_op jit(solution)/shard_map/ppermute | solution.py:61
  26.8 2.1 %collective-permute-done.10 = f32[128,256]{1,0:T(8,128)S(1)} collective-permute-done((f32[128,256]{1,0:T(8,128)S(1)}, f32[128,256]{1,0:T(8,128)S(1)}, u32[]{:S(2)}, u32[]{:S(2)}) %collective-permute-start.10) | collective-permute-done | bytes 131104 | tf_op jit(solution)/shard_map/ppermute | solution.py:61
  30.3 1.9 %collective-permute-done.11 = f32[128,256]{1,0:T(8,128)S(1)} collective-permute-done((f32[128,256]{1,0:T(8,128)S(1)}, f32[128,256]{1,0:T(8,128)S(1)}, u32[]{:S(2)}, u32[]{:S(2)}) %collective-permute-start.11) | collective-permute-done | bytes 131104 | tf_op jit(solution)/shard_map/ppermute | solution.py:61
  32.2 3.4 %collective-permute-start.12 = (f32[128,256]{1,0:T(8,128)S(1)}, f32[128,256]{1,0:T(8,128)S(1)}, u32[]{:S(2)}, u32[]{:S(2)}) collective-permute-start(f32[128,256]{1,0:T(8,128)S(1)} %add.41), channel_id=1, source_target_pairs={{0,6},{1,7},{2,0},{3,1},{4,2},{5,3},{6,4},{7,5},{8,14},{9,15},{10,... | collective-permute-start | bytes 393224 | tf_op jit(solution)/shard_map/ppermute | solution.py:61
  36.3 12.5 %collective-permute-start.3 = (f32[64,256]{1,0:T(8,128)S(1)}, f32[64,256]{1,0:T(8,128)S(1)}, u32[]{:S(2)}, u32[]{:S(2)}) collective-permute-start(f32[64,256]{1,0:T(8,128)S(1)} %get-tuple-element.59), channel_id=1, source_target_pairs={{0,0},{1,32},{2,8},{3,40},{4,16},{5,48},{6,24},{7,56},{8,1},{9,33}... | collective-permute-start | bytes 196616 | tf_op jit(solution)/shard_map/ppermute | solution.py:61
  50.1 2.7 %collective-permute-start.5 = (f32[64,256]{1,0:T(8,128)S(1)}, f32[64,256]{1,0:T(8,128)S(1)}, u32[]{:S(2)}, u32[]{:S(2)}) collective-permute-start(f32[64,256]{1,0:T(8,128)S(1)} %collective-permute-done.3), channel_id=1, source_target_pairs={{0,56},{1,57},{2,58},{3,59},{4,60},{5,61},{6,62},{7,63},{8,0},{9,1... | collective-permute-start | bytes 196616 | tf_op jit(solution)/shard_map/ppermute | solution.py:61
  55.0 3.5 %collective-permute-start.6 = (f32[3,64,256]{2,1,0:T(8,128)S(1)}, f32[3,64,256]{2,1,0:T(8,128)S(1)}, u32[]{:S(2)}, u32[]{:S(2)}) collective-permute-start(f32[3,64,256]{2,1,0:T(8,128)S(1)} %pad_maximum_fusion.1), channel_id=1, source_target_pairs={{0,24},{1,25},{2,26},{3,27},{4,28},{5,29},{6,30},{7,31},{8,32},{9,... | collective-permute-start | bytes 589832 | tf_op jit(solution)/shard_map/ppermute | solution.py:61
  59.7 2.6 %collective-permute-start.19 = (f32[256,256]{1,0:T(8,128)S(1)}, f32[256,256]{1,0:T(8,128)S(1)}, u32[]{:S(2)}, u32[]{:S(2)}) collective-permute-start(f32[256,256]{1,0:T(8,128)S(1)} %slice_select_fusion), channel_id=1, source_target_pairs={{0,2},{1,3},{8,10},{9,11},{16,18},{17,19},{24,26},{25,27},{32,34},... | collective-permute-start | bytes 786440 | tf_op jit(solution)/shard_map/ppermute | solution.py:61
  63.2 6.4 %shard_map.41 = (f32[128,128]{1,0:T(8,128)}, f32[128,128]{1,0:T(8,128)}, f32[128,128]{1,0:T(8,128)}, f32[128,128]{1,0:T(8,128)}) custom-call(f32[4,128,256]{2,1,0:T(8,128)} %copy-done, f32[4,128,256]{2,1,0:T(8,128)} %copy-done.7), custom_call_target="tpu_custom_call" | custom-call | flops 6000000000 | tf_op jit(solution)/shard_map/pallas_call | solution.py:294
  69.6 7.5 %shard_map.42 = (f32[256,256]{1,0:T(8,128)}, f32[256,256]{1,0:T(8,128)}, f32[256,256]{1,0:T(8,128)}, f32[384,128]{1,0:T(8,128)}) custom-call(f32[4,128,256]{2,1,0:T(8,128)} %copy-done, f32[4,128,256]{2,1,0:T(8,128)} %copy-done.7, f32[128,128]{1,0:T(8,128)} %get-tuple-element.30.ua_ref, f32[128,128]{1,0:T(8,128)} %get-tuple-element.31.la_ref, ...), custom_call_target="tpu_custom_call" | custom-call | flops 6000000000 | tf_op jit(solution)/shard_map/pallas_call | solution.py:294
  77.2 3.5 %collective-permute-start.22 = (f32[8,64,256]{2,1,0:T(8,128)S(1)}, f32[8,64,256]{2,1,0:T(8,128)S(1)}, u32[]{:S(2)}, u32[]{:S(2)}) collective-permute-start(f32[8,64,256]{2,1,0:T(8,128)S(1)} %constant_dynamic-update-slice_fusion.own_ref), channel_id=1, source_target_pairs={{0,192},{1,193},{2,194},{3,195},{4,196},{5,197},{6,198},{7,199},{8... | collective-permute-start | bytes 1572872 | tf_op jit(solution)/shard_map/ppermute | solution.py:61
  80.7 2.8 %collective-permute-start.20 = (f32[256,256]{1,0:T(8,128)S(1)}, f32[256,256]{1,0:T(8,128)S(1)}, u32[]{:S(2)}, u32[]{:S(2)}) collective-permute-start(f32[256,256]{1,0:T(8,128)S(1)} %add.42), channel_id=1, source_target_pairs={{0,6},{2,4},{1,7},{3,5},{8,14},{10,12},{9,15},{11,13},{16,22},{18,... | collective-permute-start | bytes 786440 | tf_op jit(solution)/shard_map/ppermute | solution.py:61
  83.5 6.2 %shard_map.43 = (f32[128,128]{1,0:T(8,128)}, f32[128,128]{1,0:T(8,128)}, f32[128,128]{1,0:T(8,128)}, f32[128,128]{1,0:T(8,128)}) custom-call(f32[384,128]{1,0:T(8,128)} %get-tuple-element.37.s_ref), custom_call_target="tpu_custom_call" | custom-call | flops 6000000000 | tf_op jit(solution)/shard_map/pallas_call | solution.py:294
  89.7 6.1 %collective-permute-start.21 = (f32[256,256]{1,0:T(8,128)S(1)}, f32[256,256]{1,0:T(8,128)S(1)}, u32[]{:S(2)}, u32[]{:S(2)}) collective-permute-start(f32[256,256]{1,0:T(8,128)S(1)} %add.43.row_ref), channel_id=1, source_target_pairs={{0,1},{1,0},{2,3},{3,2},{4,5},{5,4},{6,7},{7,6},{8,9},{9,8},{10,11... | collective-permute-start | bytes 786440 | tf_op jit(solution)/shard_map/ppermute | solution.py:61
  95.8 5.8 %shard_map.44 = (f32[256,256]{1,0:T(8,128)}, f32[256,256]{1,0:T(8,128)}) custom-call(f32[128,128]{1,0:T(8,128)} %get-tuple-element.38.ua_ref, f32[128,128]{1,0:T(8,128)} %get-tuple-element.39.la_ref, f32[128,128]{1,0:T(8,128)} %get-tuple-element.40.ub_ref, f32[128,128]{1,0:T(8,128)} %get-tuple-element.41.s_ref), custom_call_target="tpu_custom_call" | custom-call | flops 6000000000 | tf_op jit(solution)/shard_map/pallas_call | solution.py:294
  101.7 3.0 %collective-permute-start.23 = (f32[4,64,256]{2,1,0:T(8,128)S(1)}, f32[4,64,256]{2,1,0:T(8,128)S(1)}, u32[]{:S(2)}, u32[]{:S(2)}) collective-permute-start(f32[4,64,256]{2,1,0:T(8,128)S(1)} %slice.33), channel_id=1, source_target_pairs={{0,192},{1,193},{2,194},{3,195},{4,196},{5,197},{6,198},{7,199},{8... | collective-permute-start | bytes 786440 | tf_op jit(solution)/shard_map/ppermute | solution.py:61
  104.9 9.8 %shard_map.45 = (f32[256,1024]{1,0:T(8,128)}, f32[256,128]{1,0:T(8,128)}, f32[256,256]{1,0:T(8,128)}, f32[256,256]{1,0:T(8,128)}) custom-call(f32[4,128,256]{2,1,0:T(8,128)} %copy-done, f32[4,128,256]{2,1,0:T(8,128)} %copy-done.7, f32[256,1024]{1,0:T(8,128)} %a_ref.3, f32[256,128]{1,0:T(8,128)} %b_ref.1, f32[256,256]{1,0:T(8,128)} %copy-done.1, ...), custom_call_target="tpu_custom_call" | custom-call | flops 6000000000 | tf_op jit(solution)/shard_map/pallas_call | solution.py:294
  115.4 4.0 %shard_map.46 = f32[256,1024]{1,0:T(8,128)} custom-call(f32[256,1024]{1,0:T(8,128)} %a_ref.3, f32[4,64,256]{2,1,0:T(8,128)} %copy-done.3, f32[4,64,256]{2,1,0:T(8,128)} %copy-done.2, f32[256,256]{1,0:T(8,128)} %get-tuple-element.34.u0_ref, f32[256,256]{1,0:T(8,128)} %get-tuple-element.49.inv0_ref, ...), custom_call_target="tpu_custom_call", output_to_operand_aliasing={{}: (10, {})} | custom-call | tf_op jit(solution)/shard_map/pallas_call | solution.py:294
  (71 shorter events, 15.6 us)
Async XLA Ops:
  1.6 8.2 %collective-permute-start = (f32[64,256]{1,0:T(8,128)S(1)}, f32[64,256]{1,0:T(8,128)S(1)}, u32[]{:S(2)}, u32[]{:S(2)}) collective-permute-start(f32[64,256]{1,0:T(8,128)S(1)} %get-tuple-element.60), channel_id=1, source_target_pairs={{0,2},{1,3},{8,10},{9,11},{16,18},{17,19},{24,26},{25,27},{32,34},... | collective-permute-start | bytes 196616 | tf_op jit(solution)/shard_map/ppermute | solution.py:61
  5.5 4.3 %collective-permute-start.1 = (f32[64,256]{1,0:T(8,128)S(1)}, f32[64,256]{1,0:T(8,128)S(1)}, u32[]{:S(2)}, u32[]{:S(2)}) collective-permute-start(f32[64,256]{1,0:T(8,128)S(1)} %get-tuple-element.62), channel_id=1, source_target_pairs={{0,4},{1,5},{8,12},{9,13},{16,20},{17,21},{24,28},{25,29},{32,36},... | collective-permute-start | bytes 196616 | tf_op jit(solution)/shard_map/ppermute | solution.py:61
  7.7 2.6 %collective-permute-start.2 = (f32[64,256]{1,0:T(8,128)S(1)}, f32[64,256]{1,0:T(8,128)S(1)}, u32[]{:S(2)}, u32[]{:S(2)}) collective-permute-start(f32[64,256]{1,0:T(8,128)S(1)} %get-tuple-element.61), channel_id=1, source_target_pairs={{0,6},{1,7},{8,14},{9,15},{16,22},{17,23},{24,30},{25,31},{32,38},... | collective-permute-start | bytes 196616 | tf_op jit(solution)/shard_map/ppermute | solution.py:61
  11.2 5.1 %collective-permute-start.7 = (f32[128,256]{1,0:T(8,128)S(1)}, f32[128,256]{1,0:T(8,128)S(1)}, u32[]{:S(2)}, u32[]{:S(2)}) collective-permute-start(f32[128,256]{1,0:T(8,128)S(1)} %maximum_select_fusion), channel_id=1, source_target_pairs={{0,8},{2,10},{4,12},{6,14},{8,0},{10,2},{12,4},{14,6},{1,65},{3,67... | collective-permute-start | bytes 393224 | tf_op jit(solution)/shard_map/ppermute | solution.py:61
  16.4 3.2 %collective-permute-start.8 = (f32[128,256]{1,0:T(8,128)S(1)}, f32[128,256]{1,0:T(8,128)S(1)}, u32[]{:S(2)}, u32[]{:S(2)}) collective-permute-start(f32[128,256]{1,0:T(8,128)S(1)} %add.37), channel_id=1, source_target_pairs={{0,48},{2,50},{4,52},{6,54},{8,24},{10,26},{12,28},{14,30},{1,193}... | collective-permute-start | bytes 393224 | tf_op jit(solution)/shard_map/ppermute | solution.py:61
  19.6 5.9 %collective-permute-start.9 = (f32[128,256]{1,0:T(8,128)S(1)}, f32[128,256]{1,0:T(8,128)S(1)}, u32[]{:S(2)}, u32[]{:S(2)}) collective-permute-start(f32[128,256]{1,0:T(8,128)S(1)} %add.38), channel_id=1, source_target_pairs={{0,56},{2,58},{4,60},{6,62},{8,16},{10,18},{12,20},{14,22},{48,40}... | collective-permute-start | bytes 393224 | tf_op jit(solution)/shard_map/ppermute | solution.py:61
  25.5 3.4 %collective-permute-start.10 = (f32[128,256]{1,0:T(8,128)S(1)}, f32[128,256]{1,0:T(8,128)S(1)}, u32[]{:S(2)}, u32[]{:S(2)}) collective-permute-start(f32[128,256]{1,0:T(8,128)S(1)} %add.39), channel_id=1, source_target_pairs={{0,64},{2,66},{4,68},{6,70},{8,72},{10,74},{12,76},{14,78},{16,80}... | collective-permute-start | bytes 393224 | tf_op jit(solution)/shard_map/ppermute | solution.py:61
  29.0 3.2 %collective-permute-start.11 = (f32[128,256]{1,0:T(8,128)S(1)}, f32[128,256]{1,0:T(8,128)S(1)}, u32[]{:S(2)}, u32[]{:S(2)}) collective-permute-start(f32[128,256]{1,0:T(8,128)S(1)} %add.40), channel_id=1, source_target_pairs={{0,192},{2,194},{4,196},{6,198},{8,200},{10,202},{12,204},{14,206}... | collective-permute-start | bytes 393224 | tf_op jit(solution)/shard_map/ppermute | solution.py:61
  32.2 16.6 %collective-permute-start.12 = (f32[128,256]{1,0:T(8,128)S(1)}, f32[128,256]{1,0:T(8,128)S(1)}, u32[]{:S(2)}, u32[]{:S(2)}) collective-permute-start(f32[128,256]{1,0:T(8,128)S(1)} %add.41), channel_id=1, source_target_pairs={{0,6},{1,7},{2,0},{3,1},{4,2},{5,3},{6,4},{7,5},{8,14},{9,15},{10,... | collective-permute-start | bytes 393224 | tf_op jit(solution)/shard_map/ppermute | solution.py:61
  35.6 13.2 %collective-permute-start.13 = (f32[128,256]{1,0:T(8,128)S(1)}, f32[128,256]{1,0:T(8,128)S(1)}, u32[]{:S(2)}, u32[]{:S(2)}) collective-permute-start(f32[128,256]{1,0:T(8,128)S(1)} %add.41), channel_id=1, source_target_pairs={{0,4},{1,5},{2,6},{3,7},{4,0},{5,1},{6,2},{7,3},{8,12},{9,13},{10,... | collective-permute-start | bytes 393224 | tf_op jit(solution)/shard_map/ppermute | solution.py:61
  35.6 13.2 %collective-permute-start.14 = (f32[128,256]{1,0:T(8,128)S(1)}, f32[128,256]{1,0:T(8,128)S(1)}, u32[]{:S(2)}, u32[]{:S(2)}) collective-permute-start(f32[128,256]{1,0:T(8,128)S(1)} %add.41), channel_id=1, source_target_pairs={{0,2},{1,3},{2,4},{3,5},{4,6},{5,7},{6,0},{7,1},{8,10},{9,11},{10,... | collective-permute-start | bytes 393224 | tf_op jit(solution)/shard_map/ppermute | solution.py:61
  36.3 13.8 %collective-permute-start.3 = (f32[64,256]{1,0:T(8,128)S(1)}, f32[64,256]{1,0:T(8,128)S(1)}, u32[]{:S(2)}, u32[]{:S(2)}) collective-permute-start(f32[64,256]{1,0:T(8,128)S(1)} %get-tuple-element.59), channel_id=1, source_target_pairs={{0,0},{1,32},{2,8},{3,40},{4,16},{5,48},{6,24},{7,56},{8,1},{9,33}... | collective-permute-start | bytes 196616 | tf_op jit(solution)/shard_map/ppermute | solution.py:61
  48.9 13.4 %collective-permute-start.15 = (f32[4,128,256]{2,1,0:T(8,128)S(1)}, f32[4,128,256]{2,1,0:T(8,128)S(1)}, u32[]{:S(2)}, u32[]{:S(2)}) collective-permute-start(f32[4,128,256]{2,1,0:T(8,128)S(1)} %pad_maximum_fusion.mine_ref), channel_id=1, source_target_pairs={{0,1},{1,0},{2,3},{3,2},{4,5},{5,4},{6,7},{7,6},{8,9},{9,8},{10,11... | collective-permute-start | bytes 1572872 | tf_op jit(solution)/shard_map/ppermute | solution.py:61
  50.1 4.3 %collective-permute-start.4 = (f32[64,256]{1,0:T(8,128)S(1)}, f32[64,256]{1,0:T(8,128)S(1)}, u32[]{:S(2)}, u32[]{:S(2)}) collective-permute-start(f32[64,256]{1,0:T(8,128)S(1)} %collective-permute-done.3), channel_id=1, source_target_pairs={{0,8},{1,9},{2,10},{3,11},{4,12},{5,13},{6,14},{7,15},{8,16},{9,17... | collective-permute-start | bytes 196616 | tf_op jit(solution)/shard_map/ppermute | solution.py:61
  50.1 4.9 %collective-permute-start.5 = (f32[64,256]{1,0:T(8,128)S(1)}, f32[64,256]{1,0:T(8,128)S(1)}, u32[]{:S(2)}, u32[]{:S(2)}) collective-permute-start(f32[64,256]{1,0:T(8,128)S(1)} %collective-permute-done.3), channel_id=1, source_target_pairs={{0,56},{1,57},{2,58},{3,59},{4,60},{5,61},{6,62},{7,63},{8,0},{9,1... | collective-permute-start | bytes 196616 | tf_op jit(solution)/shard_map/ppermute | solution.py:61
  55.0 22.1 %collective-permute-start.6 = (f32[3,64,256]{2,1,0:T(8,128)S(1)}, f32[3,64,256]{2,1,0:T(8,128)S(1)}, u32[]{:S(2)}, u32[]{:S(2)}) collective-permute-start(f32[3,64,256]{2,1,0:T(8,128)S(1)} %pad_maximum_fusion.1), channel_id=1, source_target_pairs={{0,24},{1,25},{2,26},{3,27},{4,28},{5,29},{6,30},{7,31},{8,32},{9,... | collective-permute-start | bytes 589832 | tf_op jit(solution)/shard_map/ppermute | solution.py:61
  58.5 18.6 %collective-permute-start.16 = (f32[2,64,256]{2,1,0:T(8,128)S(1)}, f32[2,64,256]{2,1,0:T(8,128)S(1)}, u32[]{:S(2)}, u32[]{:S(2)}) collective-permute-start(f32[2,64,256]{2,1,0:T(8,128)S(1)} %pad_maximum_fusion.2), channel_id=1, source_target_pairs={{0,40},{1,41},{2,42},{3,43},{4,44},{5,45},{6,46},{7,47},{8,48},{9,... | collective-permute-start | bytes 393224 | tf_op jit(solution)/shard_map/ppermute | solution.py:61
  59.7 21.0 %collective-permute-start.19 = (f32[256,256]{1,0:T(8,128)S(1)}, f32[256,256]{1,0:T(8,128)S(1)}, u32[]{:S(2)}, u32[]{:S(2)}) collective-permute-start(f32[256,256]{1,0:T(8,128)S(1)} %slice_select_fusion), channel_id=1, source_target_pairs={{0,2},{1,3},{8,10},{9,11},{16,18},{17,19},{24,26},{25,27},{32,34},... | collective-permute-start | bytes 786440 | tf_op jit(solution)/shard_map/ppermute | solution.py:61
  77.2 24.4 %collective-permute-start.22 = (f32[8,64,256]{2,1,0:T(8,128)S(1)}, f32[8,64,256]{2,1,0:T(8,128)S(1)}, u32[]{:S(2)}, u32[]{:S(2)}) collective-permute-start(f32[8,64,256]{2,1,0:T(8,128)S(1)} %constant_dynamic-update-slice_fusion.own_ref), channel_id=1, source_target_pairs={{0,192},{1,193},{2,194},{3,195},{4,196},{5,197},{6,198},{7,199},{8... | collective-permute-start | bytes 1572872 | tf_op jit(solution)/shard_map/ppermute | solution.py:61
  80.7 21.0 %collective-permute-start.17 = (f32[8,64,256]{2,1,0:T(8,128)S(1)}, f32[8,64,256]{2,1,0:T(8,128)S(1)}, u32[]{:S(2)}, u32[]{:S(2)}) collective-permute-start(f32[8,64,256]{2,1,0:T(8,128)S(1)} %constant_dynamic-update-slice_fusion.own_ref), channel_id=1, source_target_pairs={{0,64},{1,65},{2,66},{3,67},{4,68},{5,69},{6,70},{7,71},{8,72},{9,... | collective-permute-start | bytes 1572872 | tf_op jit(solution)/shard_map/ppermute | solution.py:61
  80.7 9.0 %collective-permute-start.20 = (f32[256,256]{1,0:T(8,128)S(1)}, f32[256,256]{1,0:T(8,128)S(1)}, u32[]{:S(2)}, u32[]{:S(2)}) collective-permute-start(f32[256,256]{1,0:T(8,128)S(1)} %add.42), channel_id=1, source_target_pairs={{0,6},{2,4},{1,7},{3,5},{8,14},{10,12},{9,15},{11,13},{16,22},{18,... | collective-permute-start | bytes 786440 | tf_op jit(solution)/shard_map/ppermute | solution.py:61
  89.7 11.9 %collective-permute-start.21 = (f32[256,256]{1,0:T(8,128)S(1)}, f32[256,256]{1,0:T(8,128)S(1)}, u32[]{:S(2)}, u32[]{:S(2)}) collective-permute-start(f32[256,256]{1,0:T(8,128)S(1)} %add.43.row_ref), channel_id=1, source_target_pairs={{0,1},{1,0},{2,3},{3,2},{4,5},{5,4},{6,7},{7,6},{8,9},{9,8},{10,11... | collective-permute-start | bytes 786440 | tf_op jit(solution)/shard_map/ppermute | solution.py:61
  101.7 12.9 %collective-permute-start.23 = (f32[4,64,256]{2,1,0:T(8,128)S(1)}, f32[4,64,256]{2,1,0:T(8,128)S(1)}, u32[]{:S(2)}, u32[]{:S(2)}) collective-permute-start(f32[4,64,256]{2,1,0:T(8,128)S(1)} %slice.33), channel_id=1, source_target_pairs={{0,192},{1,193},{2,194},{3,195},{4,196},{5,197},{6,198},{7,199},{8... | collective-permute-start | bytes 786440 | tf_op jit(solution)/shard_map/ppermute | solution.py:61
  104.8 9.9 %collective-permute-start.18 = (f32[4,64,256]{2,1,0:T(8,128)S(1)}, f32[4,64,256]{2,1,0:T(8,128)S(1)}, u32[]{:S(2)}, u32[]{:S(2)}) collective-permute-start(f32[4,64,256]{2,1,0:T(8,128)S(1)} %slice.31), channel_id=1, source_target_pairs={{0,64},{1,65},{2,66},{3,67},{4,68},{5,69},{6,70},{7,71},{8,72},{9,... | collective-permute-start | bytes 786440 | tf_op jit(solution)/shard_map/ppermute | solution.py:61
  (9 other events, 45.7 us)

commit v2 on v1

--- a/solution.py
+++ b/solution.py
@@ -215,33 +215,12 @@
     return c0, c1
 
 
-def finish_tile(step, a_ref, out_ref, done_ref, sem, l0, l1, s_l0, s_l1, c0, c1, u0_ref, u1_ref):
+def update_kernel(
+    mine_ref, other_ref, a_ref, b_ref, row_ref, other_row_ref, own_ref, next_ref, far0_ref,
+    far1_ref, prev_ref, u0_ref, inv0_ref, u01_ref, u1_ref, inv1_ref,
+    out_ref, solved_ref, tile_ref, rhs_ref,
+):
     y, z, x, core = position()
-    row = y * NZ + z
-    slot = lax.rem(y + step, NY)
-    lanes = pl.ds(pl.multiple_of(slot * NB, NB), NB)
-    new = a_ref[:, lanes] - (dot3(s_l0, c0) + dot3(s_l1, c1))
-    done_ref[...] = jnp.where(row >= 2, new, 0.0)
-
-    @pl.when((slot == 0) & (x == 0) & (core == 0))
-    def _():
-        done_ref[...] = jnp.where(row == 0, u0_ref[...].T, l0)
-
-    @pl.when((slot == 0) & (x == 0) & (core == 1))
-    def _():
-        done_ref[...] = jnp.where(row == 0, 0.0, jnp.where(row == 1, u1_ref[...].T, l1))
-
-    copy = pltpu.make_async_copy(done_ref, out_ref.at[:, lanes], sem)
-    copy.start()
-    return copy
-
-
-def update_kernel(
-    mine_ref, other_ref, a_ref, b_ref, row_ref, other_row_ref, own_ref, next_ref, prev_ref,
-    u0_ref, inv0_ref, u01_ref, u1_ref, inv1_ref,
-    out_ref, solved_ref, l0_ref, l1_ref, tile_ref, rhs_ref, done_ref, sem,
-):
-    y, z, _, core = position()
     row = y * NZ + z
     row0 = jnp.where(core == 0, row_ref[...], other_row_ref[...])
     row1 = jnp.where(core == 0, other_row_ref[...], row_ref[...])
@@ -252,53 +231,43 @@
     s_l0 = split(l0)
     l1 = dot3(split(row1 - dot3(s_l0, s_u01)), s_inv1, True)
     s_l1 = split(l1)
-    l0_ref[...] = l0
-    l1_ref[...] = l1
-    copies = []
-    for n, (step, ref) in enumerate(((0, own_ref), (1, next_ref), (3, prev_ref))):
-        c0, c1 = panel_tile(ref, ref.at[4:], tile_ref, s_inv0, s_inv1, s_u01t)
-        copies.append(
-            finish_tile(
-                step, a_ref, out_ref, done_ref.at[n], sem.at[n], l0, l1, s_l0, s_l1, c0, c1,
-                u0_ref, u1_ref,
-            )
-        )
+    tiles = (
+        (0, own_ref, own_ref.at[4:]),
+        (1, next_ref, next_ref.at[4:]),
+        (3, prev_ref, prev_ref.at[4:]),
+        (2, far0_ref, far1_ref),
+    )
+    for step, low_ref, high_ref in tiles:
+        c0, c1 = panel_tile(low_ref, high_ref, tile_ref.at[step], s_inv0, s_inv1, s_u01t)
+        slot = lax.rem(y + step, NY)
+        lanes = pl.ds(pl.multiple_of(slot * NB, NB), NB)
+        new = a_ref[:, lanes] - (dot3(s_l0, c0) + dot3(s_l1, c1))
+        out_ref[:, lanes] = jnp.where(row >= 2, new, 0.0)
     unpack(mine_ref, other_ref, LOWER, 1, rhs_ref)
     y0 = dot3(s_inv0, split(rhs_ref[:, :BLK]))
     s_y0 = split(y0)
     y1 = dot3(s_inv1, split(rhs_ref[:, BLK:] - dot3(s_u01t, s_y0)))
     solved = b_ref[...] - (dot3(s_l0, s_y0) + dot3(s_l1, split(y1)))
     solved_ref[...] = jnp.where(row == 0, y0, jnp.where(row == 1, y1, solved))
-    for copy in copies:
-        copy.wait()
-
-
-def far_kernel(
-    a_ref, far0_ref, far1_ref, u0_ref, inv0_ref, u01_ref, u1_ref, inv1_ref, l0_ref, l1_ref,
-    before_ref, out_ref, tile_ref, done_ref, sem,
-):
-    del before_ref
-    l0, l1 = l0_ref[...], l1_ref[...]
-    c0, c1 = panel_tile(
-        far0_ref, far1_ref, tile_ref,
-        split(inv0_ref[...]), split(inv1_ref[...]), split(u01_ref[...].T),
-    )
-    finish_tile(
-        2, a_ref, out_ref, done_ref, sem, l0, l1, split(l0), split(l1), c0, c1, u0_ref, u1_ref
-    ).wait()
-
-
-def local(kernel, outs, *args, scratch=(), flops=0, **kwargs):
-    vmem, anywhere = pl.BlockSpec(memory_space=pltpu.VMEM), pl.BlockSpec(memory_space=pl.ANY)
-    aliased = kwargs.get("input_output_aliases", {})
+
+    @pl.when((x == 0) & (core == 0))
+    def _():
+        out_ref[:, :NB] = jnp.where(row == 0, u0_ref[...].T, l0)
+
+    @pl.when((x == 0) & (core == 1))
+    def _():
+        out_ref[:, :NB] = jnp.where(row == 0, 0.0, jnp.where(row == 1, u1_ref[...].T, l1))
+
+
+def local(kernel, outs, *args, scratch=(), flops=0):
+    vmem = pl.BlockSpec(memory_space=pltpu.VMEM)
     return pl.pallas_call(
         kernel,
-        out_shape=[jax.ShapeDtypeStruct(s[:2], jnp.float32) for s in outs],
-        in_specs=[anywhere if n in aliased else vmem for n in range(len(args))],
-        out_specs=[anywhere if len(s) > 2 else vmem for s in outs],
-        scratch_shapes=[pltpu.VMEM(s, jnp.float32) if isinstance(s, tuple) else s for s in scratch],
+        out_shape=[jax.ShapeDtypeStruct(s, jnp.float32) for s in outs],
+        in_specs=[vmem] * len(args),
+        out_specs=[vmem] * len(outs),
+        scratch_shapes=[pltpu.VMEM(s, jnp.float32) for s in scratch],
         cost_estimate=pl.CostEstimate(flops=flops, transcendentals=0, bytes_accessed=0),
-        **kwargs,
     )(*args)
 
 
@@ -347,6 +316,11 @@
         first_half0_kernel, [square] * 4, whole, other, scratch=[tile2], flops=FLOPS
     )
 
+    left3, right3 = after(left3, first[0]), after(right3, first[0])
+    own = jnp.concatenate([left3, three, right3], 0)
+    from_prev = send(own, shift(dy=1))
+    from_next = send(own, shift(dy=-1))
+
     def row_links(pairs):
         return [
             (fid(yy, zz, s, k), fid(yy, zz, d, k))
@@ -356,41 +330,29 @@
             for s, d in pairs
         ]
 
-    mine_row = after(jnp.where(x == 0, tile, 0.0), whole)
+    mine_row = after(jnp.where(x == 0, tile, 0.0), first[0])
     got_row = send(mine_row, row_links(RING4[0]))
-    mine_row = mine_row + after(got_row, first[0])
-    got_row = send(mine_row, row_links(RING4[1]))
 
     u0, inv0, u01, s11 = local(
         second_half0_kernel, [tile2, tile2, tile2, stack3],
         whole, other, *first, scratch=[tile2, tile2], flops=FLOPS,
     )
-    left3, right3 = after(left3, u0), after(right3, u0)
-    own = jnp.concatenate([left3, three, right3], 0)
-    from_prev = send(own, shift(dy=1))
-    from_next = send(own, shift(dy=-1))
     mine_row = mine_row + after(got_row, u0)
+    got_row = send(mine_row, row_links(RING4[1]))
+    second = local(first_half1_kernel, [square] * 4, s11, flops=FLOPS)
+    mine_row = mine_row + after(got_row, second[0])
     other_row = send(mine_row, SWAP)
-    second = local(first_half1_kernel, [square] * 4, s11, flops=FLOPS)
-    u1, inv1 = local(second_half1_kernel, [tile2, tile2], *second, flops=FLOPS)
-    other_row = after(other_row, u1)
-    from_prev, from_next = after(from_prev, u1), after(from_next, u1)
+    from_prev, from_next = after(from_prev, second[0]), after(from_next, second[0])
     far0 = send(from_prev[:4], shift(dy=1))
     far1 = send(from_next[4:], shift(dy=-1))
-    out, solved, l0, l1 = local(
-        update_kernel, [a.shape + ("any",), b.shape, tile2, tile2],
-        whole, other, a, b, mine_row, other_row, own, from_next, from_prev,
+    u1, inv1 = local(second_half1_kernel, [tile2, tile2], *second, flops=FLOPS)
+    other_row, far0, far1 = after(other_row, u1), after(far0, u1), after(far1, u1)
+    out, solved = local(
+        update_kernel, [a.shape, b.shape],
+        whole, other, a, b, mine_row, other_row, own, from_next, far0, far1, from_prev,
         u0, inv0, u01, u1, inv1,
-        scratch=[(2 * NB, NB), tile2, (3, NB, NB), pltpu.SemaphoreType.DMA((3,))],
-        flops=FLOPS,
-    )
-    far0, far1 = after(far0, l0), after(far1, l0)
-    out = local(
-        far_kernel, [a.shape + ("any",)],
-        a, far0, far1, u0, inv0, u01, u1, inv1, l0, l1, out,
-        scratch=[(2 * NB, NB), tile2, pltpu.SemaphoreType.DMA],
-        input_output_aliases={10: 0},
-    )[0]
+        scratch=[(NY, 2 * NB, NB), tile2], flops=FLOPS,
+    )
     return out, solved
 
 

time: 120 us -> 119 us (level)
  the two profiles are of different devices: /device:TPU:1 before, /device:TPU:2 now
where the time goes in v2:
time: 119 us; the launch traced here: 118 us
  starting transfers between devices  56.9 us (48%)
  Pallas kernels  34.7 us (29%)
  waiting for transfers between devices  19.4 us (16%)
  local copies, waits for them, and re-layouts  3.3 us (3%)
  other arithmetic  2.84 us (2%)
    ppermute x24, starting transfers between devices, send(): return lax.ppermute(value, AXES, pairs)  56.9 us
    pallas_call x5, Pallas kernels, local(): pl.pallas_call(kernel, out_shape=[jax.ShapeDtypeStruct(s, jnp.float32) fo...  34.7 us
    ppermute x24, waiting for transfers between devices, send(): return lax.ppermute(value, AXES, pairs)  19.4 us
  transfers between devices with their start and end apart: 24, of which 11 were waited for; matrix products, arithmetic and copies ran while one was open for 2% of the time, Pallas kernels for 22%

profile of v2, /device:TPU:2, one launch (start us, length us, event | category | flops | bytes accessed | tf_op | source)
XLA Modules:
  0.0 118.2 jit_solution(11995323933407911613)
XLA Ops:
  5.0 2.7 %collective-permute-done = f32[64,256]{1,0:T(8,128)S(1)} collective-permute-done((f32[64,256]{1,0:T(8,128)S(1)}, f32[64,256]{1,0:T(8,128)S(1)}, u32[]{:S(2)}, u32[]{:S(2)}) %collective-permute-start) | collective-permute-done | bytes 65568 | tf_op jit(solution)/shard_map/ppermute | solution.py:61
  8.6 3.8 %collective-permute-start.3 = (f32[128,256]{1,0:T(8,128)S(1)}, f32[128,256]{1,0:T(8,128)S(1)}, u32[]{:S(2)}, u32[]{:S(2)}) collective-permute-start(f32[128,256]{1,0:T(8,128)S(1)} %maximum_select_fusion), channel_id=1, source_target_pairs={{0,8},{2,10},{4,12},{6,14},{8,0},{10,2},{12,4},{14,6},{1,65},{3,67... | collective-permute-start | bytes 393224 | tf_op jit(solution)/shard_map/ppermute | solution.py:61
  12.5 3.0 %collective-permute-done.3 = f32[128,256]{1,0:T(8,128)S(1)} collective-permute-done((f32[128,256]{1,0:T(8,128)S(1)}, f32[128,256]{1,0:T(8,128)S(1)}, u32[]{:S(2)}, u32[]{:S(2)}) %collective-permute-start.3) | collective-permute-done | bytes 131104 | tf_op jit(solution)/shard_map/ppermute | solution.py:61
  15.5 2.0 %collective-permute-start.4 = (f32[128,256]{1,0:T(8,128)S(1)}, f32[128,256]{1,0:T(8,128)S(1)}, u32[]{:S(2)}, u32[]{:S(2)}) collective-permute-start(f32[128,256]{1,0:T(8,128)S(1)} %add.37), channel_id=1, source_target_pairs={{0,48},{2,50},{4,52},{6,54},{8,24},{10,26},{12,28},{14,30},{1,193}... | collective-permute-start | bytes 393224 | tf_op jit(solution)/shard_map/ppermute | solution.py:61
  17.6 2.5 %collective-permute-done.4 = f32[128,256]{1,0:T(8,128)S(1)} collective-permute-done((f32[128,256]{1,0:T(8,128)S(1)}, f32[128,256]{1,0:T(8,128)S(1)}, u32[]{:S(2)}, u32[]{:S(2)}) %collective-permute-start.4) | collective-permute-done | bytes 131104 | tf_op jit(solution)/shard_map/ppermute | solution.py:61
  21.4 3.0 %collective-permute-done.5 = f32[128,256]{1,0:T(8,128)S(1)} collective-permute-done((f32[128,256]{1,0:T(8,128)S(1)}, f32[128,256]{1,0:T(8,128)S(1)}, u32[]{:S(2)}, u32[]{:S(2)}) %collective-permute-start.5) | collective-permute-done | bytes 131104 | tf_op jit(solution)/shard_map/ppermute | solution.py:61
  25.7 2.5 %collective-permute-done.6 = f32[128,256]{1,0:T(8,128)S(1)} collective-permute-done((f32[128,256]{1,0:T(8,128)S(1)}, f32[128,256]{1,0:T(8,128)S(1)}, u32[]{:S(2)}, u32[]{:S(2)}) %collective-permute-start.6) | collective-permute-done | bytes 131104 | tf_op jit(solution)/shard_map/ppermute | solution.py:61
  29.5 2.5 %collective-permute-done.7 = f32[128,256]{1,0:T(8,128)S(1)} collective-permute-done((f32[128,256]{1,0:T(8,128)S(1)}, f32[128,256]{1,0:T(8,128)S(1)}, u32[]{:S(2)}, u32[]{:S(2)}) %collective-permute-start.7) | collective-permute-done | bytes 131104 | tf_op jit(solution)/shard_map/ppermute | solution.py:61
  32.0 4.8 %collective-permute-start.10 = (f32[128,256]{1,0:T(8,128)S(1)}, f32[128,256]{1,0:T(8,128)S(1)}, u32[]{:S(2)}, u32[]{:S(2)}) collective-permute-start(f32[128,256]{1,0:T(8,128)S(1)} %add.41), channel_id=1, source_target_pairs={{0,2},{1,3},{2,4},{3,5},{4,6},{5,7},{6,0},{7,1},{8,10},{9,11},{10,... | collective-permute-start | bytes 393224 | tf_op jit(solution)/shard_map/ppermute | solution.py:61
  36.8 2.2 %collective-permute-start.8 = (f32[128,256]{1,0:T(8,128)S(1)}, f32[128,256]{1,0:T(8,128)S(1)}, u32[]{:S(2)}, u32[]{:S(2)}) collective-permute-start(f32[128,256]{1,0:T(8,128)S(1)} %add.41), channel_id=1, source_target_pairs={{0,6},{1,7},{2,0},{3,1},{4,2},{5,3},{6,4},{7,5},{8,14},{9,15},{10,... | collective-permute-start | bytes 393224 | tf_op jit(solution)/shard_map/ppermute | solution.py:61
  39.0 4.5 %collective-permute-start.15 = (f32[64,256]{1,0:T(8,128)S(1)}, f32[64,256]{1,0:T(8,128)S(1)}, u32[]{:S(2)}, u32[]{:S(2)}) collective-permute-start(f32[64,256]{1,0:T(8,128)S(1)} %get-tuple-element.51), channel_id=1, source_target_pairs={{0,0},{1,32},{2,8},{3,40},{4,16},{5,48},{6,24},{7,56},{8,1},{9,33}... | collective-permute-start | bytes 196616 | tf_op jit(solution)/shard_map/ppermute | solution.py:61
  43.6 5.5 %collective-permute-start.11 = (f32[4,128,256]{2,1,0:T(8,128)S(1)}, f32[4,128,256]{2,1,0:T(8,128)S(1)}, u32[]{:S(2)}, u32[]{:S(2)}) collective-permute-start(f32[4,128,256]{2,1,0:T(8,128)S(1)} %pad_maximum_fusion.mine_ref), channel_id=1, source_target_pairs={{0,1},{1,0},{2,3},{3,2},{4,5},{5,4},{6,7},{7,6},{8,9},{9,8},{10,11... | collective-permute-start | bytes 1572872 | tf_op jit(solution)/shard_map/ppermute | solution.py:61
  50.1 4.6 %collective-permute-start.17 = (f32[64,256]{1,0:T(8,128)S(1)}, f32[64,256]{1,0:T(8,128)S(1)}, u32[]{:S(2)}, u32[]{:S(2)}) collective-permute-start(f32[64,256]{1,0:T(8,128)S(1)} %collective-permute-done.15), channel_id=1, source_target_pairs={{0,56},{1,57},{2,58},{3,59},{4,60},{5,61},{6,62},{7,63},{8,0},{9,1... | collective-permute-start | bytes 196616 | tf_op jit(solution)/shard_map/ppermute | solution.py:61
  55.9 2.1 %collective-permute-start.19 = (f32[2,64,256]{2,1,0:T(8,128)S(1)}, f32[2,64,256]{2,1,0:T(8,128)S(1)}, u32[]{:S(2)}, u32[]{:S(2)}) collective-permute-start(f32[2,64,256]{2,1,0:T(8,128)S(1)} %pad_maximum_fusion.2), channel_id=1, source_target_pairs={{0,40},{1,41},{2,42},{3,43},{4,44},{5,45},{6,46},{7,47},{8,48},{9,... | collective-permute-start | bytes 393224 | tf_op jit(solution)/shard_map/ppermute | solution.py:61
  58.8 6.3 %collective-permute-start.18 = (f32[3,64,256]{2,1,0:T(8,128)S(1)}, f32[3,64,256]{2,1,0:T(8,128)S(1)}, u32[]{:S(2)}, u32[]{:S(2)}) collective-permute-start(f32[3,64,256]{2,1,0:T(8,128)S(1)} %pad_maximum_fusion.1), channel_id=1, source_target_pairs={{0,24},{1,25},{2,26},{3,27},{4,28},{5,29},{6,30},{7,31},{8,32},{9,... | collective-permute-start | bytes 589832 | tf_op jit(solution)/shard_map/ppermute | solution.py:61
  66.0 6.4 %shard_map.41 = (f32[128,128]{1,0:T(8,128)}, f32[128,128]{1,0:T(8,128)}, f32[128,128]{1,0:T(8,128)}, f32[128,128]{1,0:T(8,128)}) custom-call(f32[4,128,256]{2,1,0:T(8,128)} %copy-done, f32[4,128,256]{2,1,0:T(8,128)} %copy-done.5), custom_call_target="tpu_custom_call" | custom-call | flops 6000000000 | tf_op jit(solution)/shard_map/pallas_call | solution.py:264
  72.8 2.7 %collective-permute-start.21 = (f32[8,64,256]{2,1,0:T(8,128)S(1)}, f32[8,64,256]{2,1,0:T(8,128)S(1)}, u32[]{:S(2)}, u32[]{:S(2)}) collective-permute-start(f32[8,64,256]{2,1,0:T(8,128)S(1)} %constant_dynamic-update-slice_fusion.own_ref), channel_id=1, source_target_pairs={{0,64},{1,65},{2,66},{3,67},{4,68},{5,69},{6,70},{7,71},{8,72},{9,... | collective-permute-start | bytes 1572872 | tf_op jit(solution)/shard_map/ppermute | solution.py:61
  76.5 1.5 %collective-permute-start.12 = (f32[256,256]{1,0:T(8,128)S(1)}, f32[256,256]{1,0:T(8,128)S(1)}, u32[]{:S(2)}, u32[]{:S(2)}) collective-permute-start(f32[256,256]{1,0:T(8,128)S(1)} %slice_select_fusion), channel_id=1, source_target_pairs={{0,2},{1,3},{8,10},{9,11},{16,18},{17,19},{24,26},{25,27},{32,34},... | collective-permute-start | bytes 786440 | tf_op jit(solution)/shard_map/ppermute | solution.py:61
  78.0 7.5 %shard_map.42 = (f32[256,256]{1,0:T(8,128)}, f32[256,256]{1,0:T(8,128)}, f32[256,256]{1,0:T(8,128)}, f32[384,128]{1,0:T(8,128)}) custom-call(f32[4,128,256]{2,1,0:T(8,128)} %copy-done, f32[4,128,256]{2,1,0:T(8,128)} %copy-done.5, f32[128,128]{1,0:T(8,128)} %get-tuple-element.26.ua_ref, f32[128,128]{1,0:T(8,128)} %get-tuple-element.28.la_ref, ...), custom_call_target="tpu_custom_call" | custom-call | flops 6000000000 | tf_op jit(solution)/shard_map/pallas_call | solution.py:264
  85.6 6.0 %collective-permute-start.13 = (f32[256,256]{1,0:T(8,128)S(1)}, f32[256,256]{1,0:T(8,128)S(1)}, u32[]{:S(2)}, u32[]{:S(2)}) collective-permute-start(f32[256,256]{1,0:T(8,128)S(1)} %add.42), channel_id=1, source_target_pairs={{0,6},{2,4},{1,7},{3,5},{8,14},{10,12},{9,15},{11,13},{16,22},{18,... | collective-permute-start | bytes 786440 | tf_op jit(solution)/shard_map/ppermute | solution.py:61
  91.6 6.2 %shard_map.43 = (f32[128,128]{1,0:T(8,128)}, f32[128,128]{1,0:T(8,128)}, f32[128,128]{1,0:T(8,128)}, f32[128,128]{1,0:T(8,128)}) custom-call(f32[384,128]{1,0:T(8,128)} %get-tuple-element.33.s_ref), custom_call_target="tpu_custom_call" | custom-call | flops 6000000000 | tf_op jit(solution)/shard_map/pallas_call | solution.py:264
  99.8 2.1 %collective-permute-start.23 = (f32[4,64,256]{2,1,0:T(8,128)S(1)}, f32[4,64,256]{2,1,0:T(8,128)S(1)}, u32[]{:S(2)}, u32[]{:S(2)}) collective-permute-start(f32[4,64,256]{2,1,0:T(8,128)S(1)} %slice.33), channel_id=1, source_target_pairs={{0,192},{1,193},{2,194},{3,195},{4,196},{5,197},{6,198},{7,199},{8... | collective-permute-start | bytes 786440 | tf_op jit(solution)/shard_map/ppermute | solution.py:61
  101.9 5.8 %shard_map.44 = (f32[256,256]{1,0:T(8,128)}, f32[256,256]{1,0:T(8,128)}) custom-call(f32[128,128]{1,0:T(8,128)} %get-tuple-element.34.ua_ref, f32[128,128]{1,0:T(8,128)} %get-tuple-element.36.la_ref, f32[128,128]{1,0:T(8,128)} %get-tuple-element.37.ub_ref, f32[128,128]{1,0:T(8,128)} %get-tuple-element.38.s_ref), custom_call_target="tpu_custom_call" | custom-call | flops 6000000000 | tf_op jit(solution)/shard_map/pallas_call | solution.py:264
  109.3 8.8 %shard_map.45 = (f32[256,1024]{1,0:T(8,128)}, f32[256,128]{1,0:T(8,128)}) custom-call(f32[4,128,256]{2,1,0:T(8,128)} %copy-done, f32[4,128,256]{2,1,0:T(8,128)} %copy-done.5, f32[256,1024]{1,0:T(8,128)} %a_ref.1, f32[256,128]{1,0:T(8,128)} %b_ref.1, f32[256,256]{1,0:T(8,128)} %copy-done.1, f32[256,256]{1,0:T(8,128)} %copy-done.6, f32[8,64,256]{2,1,0:T(8,128)} %copy-done.4, ...), custom_call_target="tpu_custom_call" | custom-call | flops 6000000000 | tf_op jit(solution)/shard_map/pallas_call | solution.py:264
  (70 shorter events, 18.2 us)
Async XLA Ops:
  1.6 6.2 %collective-permute-start = (f32[64,256]{1,0:T(8,128)S(1)}, f32[64,256]{1,0:T(8,128)S(1)}, u32[]{:S(2)}, u32[]{:S(2)}) collective-permute-start(f32[64,256]{1,0:T(8,128)S(1)} %get-tuple-element.52), channel_id=1, source_target_pairs={{0,2},{1,3},{8,10},{9,11},{16,18},{17,19},{24,26},{25,27},{32,34},... | collective-permute-start | bytes 196616 | tf_op jit(solution)/shard_map/ppermute | solution.py:61
  2.9 4.9 %collective-permute-start.2 = (f32[64,256]{1,0:T(8,128)S(1)}, f32[64,256]{1,0:T(8,128)S(1)}, u32[]{:S(2)}, u32[]{:S(2)}) collective-permute-start(f32[64,256]{1,0:T(8,128)S(1)} %get-tuple-element.53), channel_id=1, source_target_pairs={{0,6},{1,7},{8,14},{9,15},{16,22},{17,23},{24,30},{25,31},{32,38},... | collective-permute-start | bytes 196616 | tf_op jit(solution)/shard_map/ppermute | solution.py:61
  3.5 4.2 %collective-permute-start.1 = (f32[64,256]{1,0:T(8,128)S(1)}, f32[64,256]{1,0:T(8,128)S(1)}, u32[]{:S(2)}, u32[]{:S(2)}) collective-permute-start(f32[64,256]{1,0:T(8,128)S(1)} %get-tuple-element.54), channel_id=1, source_target_pairs={{0,4},{1,5},{8,12},{9,13},{16,20},{17,21},{24,28},{25,29},{32,36},... | collective-permute-start | bytes 196616 | tf_op jit(solution)/shard_map/ppermute | solution.py:61
  8.6 6.9 %collective-permute-start.3 = (f32[128,256]{1,0:T(8,128)S(1)}, f32[128,256]{1,0:T(8,128)S(1)}, u32[]{:S(2)}, u32[]{:S(2)}) collective-permute-start(f32[128,256]{1,0:T(8,128)S(1)} %maximum_select_fusion), channel_id=1, source_target_pairs={{0,8},{2,10},{4,12},{6,14},{8,0},{10,2},{12,4},{14,6},{1,65},{3,67... | collective-permute-start | bytes 393224 | tf_op jit(solution)/shard_map/ppermute | solution.py:61
  15.5 4.5 %collective-permute-start.4 = (f32[128,256]{1,0:T(8,128)S(1)}, f32[128,256]{1,0:T(8,128)S(1)}, u32[]{:S(2)}, u32[]{:S(2)}) collective-permute-start(f32[128,256]{1,0:T(8,128)S(1)} %add.37), channel_id=1, source_target_pairs={{0,48},{2,50},{4,52},{6,54},{8,24},{10,26},{12,28},{14,30},{1,193}... | collective-permute-start | bytes 393224 | tf_op jit(solution)/shard_map/ppermute | solution.py:61
  20.1 4.3 %collective-permute-start.5 = (f32[128,256]{1,0:T(8,128)S(1)}, f32[128,256]{1,0:T(8,128)S(1)}, u32[]{:S(2)}, u32[]{:S(2)}) collective-permute-start(f32[128,256]{1,0:T(8,128)S(1)} %add.38), channel_id=1, source_target_pairs={{0,56},{2,58},{4,60},{6,62},{8,16},{10,18},{12,20},{14,22},{48,40}... | collective-permute-start | bytes 393224 | tf_op jit(solution)/shard_map/ppermute | solution.py:61
  24.4 3.8 %collective-permute-start.6 = (f32[128,256]{1,0:T(8,128)S(1)}, f32[128,256]{1,0:T(8,128)S(1)}, u32[]{:S(2)}, u32[]{:S(2)}) collective-permute-start(f32[128,256]{1,0:T(8,128)S(1)} %add.39), channel_id=1, source_target_pairs={{0,64},{2,66},{4,68},{6,70},{8,72},{10,74},{12,76},{14,78},{16,80}... | collective-permute-start | bytes 393224 | tf_op jit(solution)/shard_map/ppermute | solution.py:61
  28.2 3.8 %collective-permute-start.7 = (f32[128,256]{1,0:T(8,128)S(1)}, f32[128,256]{1,0:T(8,128)S(1)}, u32[]{:S(2)}, u32[]{:S(2)}) collective-permute-start(f32[128,256]{1,0:T(8,128)S(1)} %add.40), channel_id=1, source_target_pairs={{0,192},{2,194},{4,196},{6,198},{8,200},{10,202},{12,204},{14,206}... | collective-permute-start | bytes 393224 | tf_op jit(solution)/shard_map/ppermute | solution.py:61
  32.0 11.5 %collective-permute-start.10 = (f32[128,256]{1,0:T(8,128)S(1)}, f32[128,256]{1,0:T(8,128)S(1)}, u32[]{:S(2)}, u32[]{:S(2)}) collective-permute-start(f32[128,256]{1,0:T(8,128)S(1)} %add.41), channel_id=1, source_target_pairs={{0,2},{1,3},{2,4},{3,5},{4,6},{5,7},{6,0},{7,1},{8,10},{9,11},{10,... | collective-permute-start | bytes 393224 | tf_op jit(solution)/shard_map/ppermute | solution.py:61
  36.8 6.7 %collective-permute-start.9 = (f32[128,256]{1,0:T(8,128)S(1)}, f32[128,256]{1,0:T(8,128)S(1)}, u32[]{:S(2)}, u32[]{:S(2)}) collective-permute-start(f32[128,256]{1,0:T(8,128)S(1)} %add.41), channel_id=1, source_target_pairs={{0,4},{1,5},{2,6},{3,7},{4,0},{5,1},{6,2},{7,3},{8,12},{9,13},{10,... | collective-permute-start | bytes 393224 | tf_op jit(solution)/shard_map/ppermute | solution.py:61
  36.8 6.7 %collective-permute-start.8 = (f32[128,256]{1,0:T(8,128)S(1)}, f32[128,256]{1,0:T(8,128)S(1)}, u32[]{:S(2)}, u32[]{:S(2)}) collective-permute-start(f32[128,256]{1,0:T(8,128)S(1)} %add.41), channel_id=1, source_target_pairs={{0,6},{1,7},{2,0},{3,1},{4,2},{5,3},{6,4},{7,5},{8,14},{9,15},{10,... | collective-permute-start | bytes 393224 | tf_op jit(solution)/shard_map/ppermute | solution.py:61
  39.0 10.1 %collective-permute-start.15 = (f32[64,256]{1,0:T(8,128)S(1)}, f32[64,256]{1,0:T(8,128)S(1)}, u32[]{:S(2)}, u32[]{:S(2)}) collective-permute-start(f32[64,256]{1,0:T(8,128)S(1)} %get-tuple-element.51), channel_id=1, source_target_pairs={{0,0},{1,32},{2,8},{3,40},{4,16},{5,48},{6,24},{7,56},{8,1},{9,33}... | collective-permute-start | bytes 196616 | tf_op jit(solution)/shard_map/ppermute | solution.py:61
  43.6 21.6 %collective-permute-start.11 = (f32[4,128,256]{2,1,0:T(8,128)S(1)}, f32[4,128,256]{2,1,0:T(8,128)S(1)}, u32[]{:S(2)}, u32[]{:S(2)}) collective-permute-start(f32[4,128,256]{2,1,0:T(8,128)S(1)} %pad_maximum_fusion.mine_ref), channel_id=1, source_target_pairs={{0,1},{1,0},{2,3},{3,2},{4,5},{5,4},{6,7},{7,6},{8,9},{9,8},{10,11... | collective-permute-start | bytes 1572872 | tf_op jit(solution)/shard_map/ppermute | solution.py:61
  49.1 6.8 %collective-permute-start.16 = (f32[64,256]{1,0:T(8,128)S(1)}, f32[64,256]{1,0:T(8,128)S(1)}, u32[]{:S(2)}, u32[]{:S(2)}) collective-permute-start(f32[64,256]{1,0:T(8,128)S(1)} %collective-permute-done.15), channel_id=1, source_target_pairs={{0,8},{1,9},{2,10},{3,11},{4,12},{5,13},{6,14},{7,15},{8,16},{9,17... | collective-permute-start | bytes 196616 | tf_op jit(solution)/shard_map/ppermute | solution.py:61
  50.1 8.7 %collective-permute-start.17 = (f32[64,256]{1,0:T(8,128)S(1)}, f32[64,256]{1,0:T(8,128)S(1)}, u32[]{:S(2)}, u32[]{:S(2)}) collective-permute-start(f32[64,256]{1,0:T(8,128)S(1)} %collective-permute-done.15), channel_id=1, source_target_pairs={{0,56},{1,57},{2,58},{3,59},{4,60},{5,61},{6,62},{7,63},{8,0},{9,1... | collective-permute-start | bytes 196616 | tf_op jit(solution)/shard_map/ppermute | solution.py:61
  55.9 16.5 %collective-permute-start.19 = (f32[2,64,256]{2,1,0:T(8,128)S(1)}, f32[2,64,256]{2,1,0:T(8,128)S(1)}, u32[]{:S(2)}, u32[]{:S(2)}) collective-permute-start(f32[2,64,256]{2,1,0:T(8,128)S(1)} %pad_maximum_fusion.2), channel_id=1, source_target_pairs={{0,40},{1,41},{2,42},{3,43},{4,44},{5,45},{6,46},{7,47},{8,48},{9,... | collective-permute-start | bytes 393224 | tf_op jit(solution)/shard_map/ppermute | solution.py:61
  58.8 13.9 %collective-permute-start.18 = (f32[3,64,256]{2,1,0:T(8,128)S(1)}, f32[3,64,256]{2,1,0:T(8,128)S(1)}, u32[]{:S(2)}, u32[]{:S(2)}) collective-permute-start(f32[3,64,256]{2,1,0:T(8,128)S(1)} %pad_maximum_fusion.1), channel_id=1, source_target_pairs={{0,24},{1,25},{2,26},{3,27},{4,28},{5,29},{6,30},{7,31},{8,32},{9,... | collective-permute-start | bytes 589832 | tf_op jit(solution)/shard_map/ppermute | solution.py:61
  72.8 25.1 %collective-permute-start.21 = (f32[8,64,256]{2,1,0:T(8,128)S(1)}, f32[8,64,256]{2,1,0:T(8,128)S(1)}, u32[]{:S(2)}, u32[]{:S(2)}) collective-permute-start(f32[8,64,256]{2,1,0:T(8,128)S(1)} %constant_dynamic-update-slice_fusion.own_ref), channel_id=1, source_target_pairs={{0,64},{1,65},{2,66},{3,67},{4,68},{5,69},{6,70},{7,71},{8,72},{9,... | collective-permute-start | bytes 1572872 | tf_op jit(solution)/shard_map/ppermute | solution.py:61
  75.5 22.4 %collective-permute-start.20 = (f32[8,64,256]{2,1,0:T(8,128)S(1)}, f32[8,64,256]{2,1,0:T(8,128)S(1)}, u32[]{:S(2)}, u32[]{:S(2)}) collective-permute-start(f32[8,64,256]{2,1,0:T(8,128)S(1)} %constant_dynamic-update-slice_fusion.own_ref), channel_id=1, source_target_pairs={{0,192},{1,193},{2,194},{3,195},{4,196},{5,197},{6,198},{7,199},{8... | collective-permute-start | bytes 1572872 | tf_op jit(solution)/shard_map/ppermute | solution.py:61
  76.5 9.0 %collective-permute-start.12 = (f32[256,256]{1,0:T(8,128)S(1)}, f32[256,256]{1,0:T(8,128)S(1)}, u32[]{:S(2)}, u32[]{:S(2)}) collective-permute-start(f32[256,256]{1,0:T(8,128)S(1)} %slice_select_fusion), channel_id=1, source_target_pairs={{0,2},{1,3},{8,10},{9,11},{16,18},{17,19},{24,26},{25,27},{32,34},... | collective-permute-start | bytes 786440 | tf_op jit(solution)/shard_map/ppermute | solution.py:61
  85.6 12.2 %collective-permute-start.13 = (f32[256,256]{1,0:T(8,128)S(1)}, f32[256,256]{1,0:T(8,128)S(1)}, u32[]{:S(2)}, u32[]{:S(2)}) collective-permute-start(f32[256,256]{1,0:T(8,128)S(1)} %add.42), channel_id=1, source_target_pairs={{0,6},{2,4},{1,7},{3,5},{8,14},{10,12},{9,15},{11,13},{16,22},{18,... | collective-permute-start | bytes 786440 | tf_op jit(solution)/shard_map/ppermute | solution.py:61
  97.8 10.0 %collective-permute-start.14 = (f32[256,256]{1,0:T(8,128)S(1)}, f32[256,256]{1,0:T(8,128)S(1)}, u32[]{:S(2)}, u32[]{:S(2)}) collective-permute-start(f32[256,256]{1,0:T(8,128)S(1)} %add.43.row_ref), channel_id=1, source_target_pairs={{0,1},{1,0},{2,3},{3,2},{4,5},{5,4},{6,7},{7,6},{8,9},{9,8},{10,11... | collective-permute-start | bytes 786440 | tf_op jit(solution)/shard_map/ppermute | solution.py:61
  98.7 9.9 %collective-permute-start.22 = (f32[4,64,256]{2,1,0:T(8,128)S(1)}, f32[4,64,256]{2,1,0:T(8,128)S(1)}, u32[]{:S(2)}, u32[]{:S(2)}) collective-permute-start(f32[4,64,256]{2,1,0:T(8,128)S(1)} %slice.32), channel_id=1, source_target_pairs={{0,64},{1,65},{2,66},{3,67},{4,68},{5,69},{6,70},{7,71},{8,72},{9,... | collective-permute-start | bytes 786440 | tf_op jit(solution)/shard_map/ppermute | solution.py:61
  99.8 8.7 %collective-permute-start.23 = (f32[4,64,256]{2,1,0:T(8,128)S(1)}, f32[4,64,256]{2,1,0:T(8,128)S(1)}, u32[]{:S(2)}, u32[]{:S(2)}) collective-permute-start(f32[4,64,256]{2,1,0:T(8,128)S(1)} %slice.33), channel_id=1, source_target_pairs={{0,192},{1,193},{2,194},{3,195},{4,196},{5,197},{6,198},{7,199},{8... | collective-permute-start | bytes 786440 | tf_op jit(solution)/shard_map/ppermute | solution.py:61
  (9 other events, 42.4 us)

commit v3 on v2

--- a/solution.py
+++ b/solution.py
@@ -132,9 +132,10 @@
 
 
 def dot3(a, b, transposed=False):
+    lhs = jnp.concatenate([a[0], a[0], a[1]], 1)
+    rhs = jnp.concatenate([b[0], b[1], b[0]], 1 if transposed else 0)
     dims = (((1,), (1 if transposed else 0,)), ((), ()))
-    prod = lambda p, q: lax.dot_general(p, q, dims, preferred_element_type=jnp.float32)
-    return prod(a[0], b[0]) + (prod(a[0], b[1]) + prod(a[1], b[0]))
+    return lax.dot_general(lhs, rhs, dims, preferred_element_type=jnp.float32)
 
 
 def position():
@@ -231,6 +232,7 @@
     s_l0 = split(l0)
     l1 = dot3(split(row1 - dot3(s_l0, s_u01)), s_inv1, True)
     s_l1 = split(l1)
+    s_l = tuple(jnp.concatenate([p, q], 1) for p, q in zip(s_l0, s_l1))
     tiles = (
         (0, own_ref, own_ref.at[4:]),
         (1, next_ref, next_ref.at[4:]),
@@ -241,7 +243,8 @@
         c0, c1 = panel_tile(low_ref, high_ref, tile_ref.at[step], s_inv0, s_inv1, s_u01t)
         slot = lax.rem(y + step, NY)
         lanes = pl.ds(pl.multiple_of(slot * NB, NB), NB)
-        new = a_ref[:, lanes] - (dot3(s_l0, c0) + dot3(s_l1, c1))
+        c = tuple(jnp.concatenate([p, q], 0) for p, q in zip(c0, c1))
+        new = a_ref[:, lanes] - dot3(s_l, c)
         out_ref[:, lanes] = jnp.where(row >= 2, new, 0.0)
     unpack(mine_ref, other_ref, LOWER, 1, rhs_ref)
     y0 = dot3(s_inv0, split(rhs_ref[:, :BLK]))
@@ -259,15 +262,18 @@
         out_ref[:, :NB] = jnp.where(row == 0, 0.0, jnp.where(row == 1, u1_ref[...].T, l1))
 
 
-def local(kernel, outs, *args, scratch=(), flops=0):
+def local(kernel, outs, *args, scratch=(), flops=0, last=False):
     vmem = pl.BlockSpec(memory_space=pltpu.VMEM)
+    args = [pltpu.with_memory_space_constraint(v, pltpu.VMEM) for v in args]
+    kept = jax.ShapeDtypeStruct if last else pltpu.VMEM
     return pl.pallas_call(
         kernel,
-        out_shape=[jax.ShapeDtypeStruct(s, jnp.float32) for s in outs],
+        out_shape=[kept(s, jnp.float32) for s in outs],
         in_specs=[vmem] * len(args),
         out_specs=[vmem] * len(outs),
         scratch_shapes=[pltpu.VMEM(s, jnp.float32) for s in scratch],
         cost_estimate=pl.CostEstimate(flops=flops, transcendentals=0, bytes_accessed=0),
+        compiler_params=pltpu.CompilerParams(vmem_limit_bytes=24 << 20),
     )(*args)
 
 
@@ -351,7 +357,7 @@
         update_kernel, [a.shape, b.shape],
         whole, other, a, b, mine_row, other_row, own, from_next, far0, far1, from_prev,
         u0, inv0, u01, u1, inv1,
-        scratch=[(NY, 2 * NB, NB), tile2], flops=FLOPS,
+        scratch=[(NY, 2 * NB, NB), tile2], flops=FLOPS, last=True,
     )
     return out, solved
 

time: 119 us -> 108 us (0.908)
  the two profiles are of different devices: /device:TPU:2 before, /device:TPU:1 now
where the time goes in v3:
time: 108 us; the launch traced here: 107 us
  starting transfers between devices  57.6 us (53%)
  Pallas kernels  25.2 us (23%)
  waiting for transfers between devices  21.5 us (20%)
  other arithmetic  1.14 us (1%)
    ppermute x24, starting transfers between devices, send(): return lax.ppermute(value, AXES, pairs)  57.6 us
    pallas_call x5, Pallas kernels, local(): pl.pallas_call(kernel, out_shape=[kept(s, jnp.float32) for s in outs], in...  25.2 us
    ppermute x24, waiting for transfers between devices, send(): return lax.ppermute(value, AXES, pairs)  21.5 us
  transfers between devices with their start and end apart: 24, of which 11 were waited for; matrix products, arithmetic and copies ran while one was open for 0% of the time, Pallas kernels for 18%

profile of v3, /device:TPU:1, one launch (start us, length us, event | category | flops | bytes accessed | tf_op | source)
XLA Modules:
  0.0 107.5 jit_solution(11479539430658828746)
XLA Ops:
  1.6 3.9 %collective-permute-start = (f32[64,256]{1,0:T(8,128)S(1)}, f32[64,256]{1,0:T(8,128)S(1)}, u32[]{:S(2)}, u32[]{:S(2)}) collective-permute-start(f32[64,256]{1,0:T(8,128)S(1)} %get-tuple-element.52), channel_id=1, source_target_pairs={{0,2},{1,3},{8,10},{9,11},{16,18},{17,19},{24,26},{25,27},{32,34},... | collective-permute-start | bytes 196616 | tf_op jit(solution)/shard_map/ppermute | solution.py:61
  5.5 1.9 %collective-permute-start.2 = (f32[64,256]{1,0:T(8,128)S(1)}, f32[64,256]{1,0:T(8,128)S(1)}, u32[]{:S(2)}, u32[]{:S(2)}) collective-permute-start(f32[64,256]{1,0:T(8,128)S(1)} %get-tuple-element.53), channel_id=1, source_target_pairs={{0,6},{1,7},{8,14},{9,15},{16,22},{17,23},{24,30},{25,31},{32,38},... | collective-permute-start | bytes 196616 | tf_op jit(solution)/shard_map/ppermute | solution.py:61
  11.0 3.2 %collective-permute-start.3 = (f32[128,256]{1,0:T(8,128)S(1)}, f32[128,256]{1,0:T(8,128)S(1)}, u32[]{:S(2)}, u32[]{:S(2)}) collective-permute-start(f32[128,256]{1,0:T(8,128)S(1)} %maximum_select_fusion), channel_id=1, source_target_pairs={{0,8},{2,10},{4,12},{6,14},{8,0},{10,2},{12,4},{14,6},{1,65},{3,67... | collective-permute-start | bytes 393224 | tf_op jit(solution)/shard_map/ppermute | solution.py:61
  14.2 1.9 %collective-permute-done.3 = f32[128,256]{1,0:T(8,128)S(1)} collective-permute-done((f32[128,256]{1,0:T(8,128)S(1)}, f32[128,256]{1,0:T(8,128)S(1)}, u32[]{:S(2)}, u32[]{:S(2)}) %collective-permute-start.3) | collective-permute-done | bytes 131104 | tf_op jit(solution)/shard_map/ppermute | solution.py:61
  17.5 1.9 %collective-permute-done.4 = f32[128,256]{1,0:T(8,128)S(1)} collective-permute-done((f32[128,256]{1,0:T(8,128)S(1)}, f32[128,256]{1,0:T(8,128)S(1)}, u32[]{:S(2)}, u32[]{:S(2)}) %collective-permute-start.4) | collective-permute-done | bytes 131104 | tf_op jit(solution)/shard_map/ppermute | solution.py:61
  19.4 3.7 %collective-permute-start.5 = (f32[128,256]{1,0:T(8,128)S(1)}, f32[128,256]{1,0:T(8,128)S(1)}, u32[]{:S(2)}, u32[]{:S(2)}) collective-permute-start(f32[128,256]{1,0:T(8,128)S(1)} %add.38), channel_id=1, source_target_pairs={{0,56},{2,58},{4,60},{6,62},{8,16},{10,18},{12,20},{14,22},{48,40}... | collective-permute-start | bytes 393224 | tf_op jit(solution)/shard_map/ppermute | solution.py:61
  23.1 2.3 %collective-permute-done.5 = f32[128,256]{1,0:T(8,128)S(1)} collective-permute-done((f32[128,256]{1,0:T(8,128)S(1)}, f32[128,256]{1,0:T(8,128)S(1)}, u32[]{:S(2)}, u32[]{:S(2)}) %collective-permute-start.5) | collective-permute-done | bytes 131104 | tf_op jit(solution)/shard_map/ppermute | solution.py:61
  26.8 2.1 %collective-permute-done.6 = f32[128,256]{1,0:T(8,128)S(1)} collective-permute-done((f32[128,256]{1,0:T(8,128)S(1)}, f32[128,256]{1,0:T(8,128)S(1)}, u32[]{:S(2)}, u32[]{:S(2)}) %collective-permute-start.6) | collective-permute-done | bytes 131104 | tf_op jit(solution)/shard_map/ppermute | solution.py:61
  30.2 1.9 %collective-permute-done.7 = f32[128,256]{1,0:T(8,128)S(1)} collective-permute-done((f32[128,256]{1,0:T(8,128)S(1)}, f32[128,256]{1,0:T(8,128)S(1)}, u32[]{:S(2)}, u32[]{:S(2)}) %collective-permute-start.7) | collective-permute-done | bytes 131104 | tf_op jit(solution)/shard_map/ppermute | solution.py:61
  32.3 3.7 %collective-permute-start.9 = (f32[128,256]{1,0:T(8,128)S(1)}, f32[128,256]{1,0:T(8,128)S(1)}, u32[]{:S(2)}, u32[]{:S(2)}) collective-permute-start(f32[128,256]{1,0:T(8,128)S(1)} %add.41), channel_id=1, source_target_pairs={{0,4},{1,5},{2,6},{3,7},{4,0},{5,1},{6,2},{7,3},{8,12},{9,13},{10,... | collective-permute-start | bytes 393224 | tf_op jit(solution)/shard_map/ppermute | solution.py:61
  35.9 2.0 %collective-permute-start.8 = (f32[128,256]{1,0:T(8,128)S(1)}, f32[128,256]{1,0:T(8,128)S(1)}, u32[]{:S(2)}, u32[]{:S(2)}) collective-permute-start(f32[128,256]{1,0:T(8,128)S(1)} %add.41), channel_id=1, source_target_pairs={{0,6},{1,7},{2,0},{3,1},{4,2},{5,3},{6,4},{7,5},{8,14},{9,15},{10,... | collective-permute-start | bytes 393224 | tf_op jit(solution)/shard_map/ppermute | solution.py:61
  37.9 12.8 %collective-permute-start.15 = (f32[64,256]{1,0:T(8,128)S(1)}, f32[64,256]{1,0:T(8,128)S(1)}, u32[]{:S(2)}, u32[]{:S(2)}) collective-permute-start(f32[64,256]{1,0:T(8,128)S(1)} %get-tuple-element.51), channel_id=1, source_target_pairs={{0,0},{1,32},{2,8},{3,40},{4,16},{5,48},{6,24},{7,56},{8,1},{9,33}... | collective-permute-start | bytes 196616 | tf_op jit(solution)/shard_map/ppermute | solution.py:61
  52.1 2.7 %collective-permute-start.17 = (f32[64,256]{1,0:T(8,128)S(1)}, f32[64,256]{1,0:T(8,128)S(1)}, u32[]{:S(2)}, u32[]{:S(2)}) collective-permute-start(f32[64,256]{1,0:T(8,128)S(1)} %collective-permute-done.15), channel_id=1, source_target_pairs={{0,56},{1,57},{2,58},{3,59},{4,60},{5,61},{6,62},{7,63},{8,0},{9,1... | collective-permute-start | bytes 196616 | tf_op jit(solution)/shard_map/ppermute | solution.py:61
  54.8 2.1 %collective-permute-done.16 = f32[64,256]{1,0:T(8,128)S(1)} collective-permute-done((f32[64,256]{1,0:T(8,128)S(1)}, f32[64,256]{1,0:T(8,128)S(1)}, u32[]{:S(2)}, u32[]{:S(2)}) %collective-permute-start.16) | collective-permute-done | bytes 65568 | tf_op jit(solution)/shard_map/ppermute | solution.py:61
  57.0 3.3 %collective-permute-start.18 = (f32[3,64,256]{2,1,0:T(8,128)S(1)}, f32[3,64,256]{2,1,0:T(8,128)S(1)}, u32[]{:S(2)}, u32[]{:S(2)}) collective-permute-start(f32[3,64,256]{2,1,0:T(8,128)S(1)} %pad_maximum_fusion.1), channel_id=1, source_target_pairs={{0,24},{1,25},{2,26},{3,27},{4,28},{5,29},{6,30},{7,31},{8,32},{9,... | collective-permute-start | bytes 589832 | tf_op jit(solution)/shard_map/ppermute | solution.py:61
  60.4 4.6 %shard_map.41 = (f32[128,128]{1,0:T(8,128)S(1)}, f32[128,128]{1,0:T(8,128)S(1)}, f32[128,128]{1,0:T(8,128)S(1)}, f32[128,128]{1,0:T(8,128)S(1)}) custom-call(f32[4,128,256]{2,1,0:T(8,128)S(1)} %pad_maximum_fusion.mine_ref, f32[4,128,256]{2,1,0:T(8,128)S(1)} %collective-permute-done.11.other_ref), custom_call_target="tpu_custom_call" | custom-call | flops 6000000000 | tf_op jit(solution)/shard_map/pallas_call | solution.py:269
  65.0 4.6 %collective-permute-done.19 = f32[2,64,256]{2,1,0:T(8,128)S(1)} collective-permute-done((f32[2,64,256]{2,1,0:T(8,128)S(1)}, f32[2,64,256]{2,1,0:T(8,128)S(1)}, u32[]{:S(2)}, u32[]{:S(2)}) %collective-permute-start.19) | collective-permute-done | bytes 131104 | tf_op jit(solution)/shard_map/ppermute | solution.py:61
  70.8 1.6 %collective-permute-start.20 = (f32[8,64,256]{2,1,0:T(8,128)S(1)}, f32[8,64,256]{2,1,0:T(8,128)S(1)}, u32[]{:S(2)}, u32[]{:S(2)}) collective-permute-start(f32[8,64,256]{2,1,0:T(8,128)S(1)} %constant_dynamic-update-slice_fusion.own_ref), channel_id=1, source_target_pairs={{0,192},{1,193},{2,194},{3,195},{4,196},{5,197},{6,198},{7,199},{8... | collective-permute-start | bytes 1572872 | tf_op jit(solution)/shard_map/ppermute | solution.py:61
  73.9 5.5 %shard_map.42 = (f32[256,256]{1,0:T(8,128)S(1)}, f32[256,256]{1,0:T(8,128)S(1)}, f32[256,256]{1,0:T(8,128)S(1)}, f32[384,128]{1,0:T(8,128)S(1)}) custom-call(f32[4,128,256]{2,1,0:T(8,128)S(1)} %pad_maximum_fusion.mine_ref, f32[4,128,256]{2,1,0:T(8,128)S(1)} %collective-permute-done.11.other_ref, f32[128,128]{1,0:T(8,128)S(1)} %get-tuple-element.26.ua_ref, ...), custom_call_target="tpu_custom_call" | custom-call | flops 6000000000 | tf_op jit(solution)/shard_map/pallas_call | solution.py:269
  80.8 4.6 %shard_map.43 = (f32[128,128]{1,0:T(8,128)S(1)}, f32[128,128]{1,0:T(8,128)S(1)}, f32[128,128]{1,0:T(8,128)S(1)}, f32[128,128]{1,0:T(8,128)S(1)}) custom-call(f32[384,128]{1,0:T(8,128)S(1)} %get-tuple-element.33.s_ref), custom_call_target="tpu_custom_call" | custom-call | flops 6000000000 | tf_op jit(solution)/shard_map/pallas_call | solution.py:269
  85.5 6.6 %collective-permute-start.14 = (f32[256,256]{1,0:T(8,128)S(1)}, f32[256,256]{1,0:T(8,128)S(1)}, u32[]{:S(2)}, u32[]{:S(2)}) collective-permute-start(f32[256,256]{1,0:T(8,128)S(1)} %add.43.row_ref), channel_id=1, source_target_pairs={{0,1},{1,0},{2,3},{3,2},{4,5},{5,4},{6,7},{7,6},{8,9},{9,8},{10,11... | collective-permute-start | bytes 786440 | tf_op jit(solution)/shard_map/ppermute | solution.py:61
  92.7 2.1 %collective-permute-start.23 = (f32[4,64,256]{2,1,0:T(8,128)S(1)}, f32[4,64,256]{2,1,0:T(8,128)S(1)}, u32[]{:S(2)}, u32[]{:S(2)}) collective-permute-start(f32[4,64,256]{2,1,0:T(8,128)S(1)} %slice.33), channel_id=1, source_target_pairs={{0,192},{1,193},{2,194},{3,195},{4,196},{5,197},{6,198},{7,199},{8... | collective-permute-start | bytes 786440 | tf_op jit(solution)/shard_map/ppermute | solution.py:61
  94.9 4.2 %shard_map.44 = (f32[256,256]{1,0:T(8,128)S(1)}, f32[256,256]{1,0:T(8,128)S(1)}) custom-call(f32[128,128]{1,0:T(8,128)S(1)} %get-tuple-element.34.ua_ref, f32[128,128]{1,0:T(8,128)S(1)} %get-tuple-element.36.la_ref, f32[128,128]{1,0:T(8,128)S(1)} %get-tuple-element.37.ub_ref, f32[128,128]{1,0:T(8,128)S(1)} %get-tuple-element.38.s_ref), custom_call_target="tpu_custom_call" | custom-call | flops 6000000000 | tf_op jit(solution)/shard_map/pallas_call | solution.py:269
  101.2 6.3 %shard_map.45 = (f32[256,1024]{1,0:T(8,128)}, f32[256,128]{1,0:T(8,128)}) custom-call(f32[4,128,256]{2,1,0:T(8,128)S(1)} %pad_maximum_fusion.mine_ref, f32[4,128,256]{2,1,0:T(8,128)S(1)} %collective-permute-done.11.other_ref, f32[256,1024]{1,0:T(8,128)S(1)} %copy-done, f32[256,128]{1,0:T(8,128)S(1)} %copy-done.1, f32[256,256]{1,0:T(8,128)S(1)} %add.43.row_ref, ...), custom_call_target="tpu_custom_call" | custom-call | flops 6000000000 | tf_op jit(solution)/shard_map/pallas_call | solution.py:269
  (56 shorter events, 16.7 us)
Async XLA Ops:
  1.6 7.2 %collective-permute-start = (f32[64,256]{1,0:T(8,128)S(1)}, f32[64,256]{1,0:T(8,128)S(1)}, u32[]{:S(2)}, u32[]{:S(2)}) collective-permute-start(f32[64,256]{1,0:T(8,128)S(1)} %get-tuple-element.52), channel_id=1, source_target_pairs={{0,2},{1,3},{8,10},{9,11},{16,18},{17,19},{24,26},{25,27},{32,34},... | collective-permute-start | bytes 196616 | tf_op jit(solution)/shard_map/ppermute | solution.py:61
  5.5 3.3 %collective-permute-start.2 = (f32[64,256]{1,0:T(8,128)S(1)}, f32[64,256]{1,0:T(8,128)S(1)}, u32[]{:S(2)}, u32[]{:S(2)}) collective-permute-start(f32[64,256]{1,0:T(8,128)S(1)} %get-tuple-element.53), channel_id=1, source_target_pairs={{0,6},{1,7},{8,14},{9,15},{16,22},{17,23},{24,30},{25,31},{32,38},... | collective-permute-start | bytes 196616 | tf_op jit(solution)/shard_map/ppermute | solution.py:61
  7.5 2.6 %collective-permute-start.1 = (f32[64,256]{1,0:T(8,128)S(1)}, f32[64,256]{1,0:T(8,128)S(1)}, u32[]{:S(2)}, u32[]{:S(2)}) collective-permute-start(f32[64,256]{1,0:T(8,128)S(1)} %get-tuple-element.54), channel_id=1, source_target_pairs={{0,4},{1,5},{8,12},{9,13},{16,20},{17,21},{24,28},{25,29},{32,36},... | collective-permute-start | bytes 196616 | tf_op jit(solution)/shard_map/ppermute | solution.py:61
  11.0 5.1 %collective-permute-start.3 = (f32[128,256]{1,0:T(8,128)S(1)}, f32[128,256]{1,0:T(8,128)S(1)}, u32[]{:S(2)}, u32[]{:S(2)}) collective-permute-start(f32[128,256]{1,0:T(8,128)S(1)} %maximum_select_fusion), channel_id=1, source_target_pairs={{0,8},{2,10},{4,12},{6,14},{8,0},{10,2},{12,4},{14,6},{1,65},{3,67... | collective-permute-start | bytes 393224 | tf_op jit(solution)/shard_map/ppermute | solution.py:61
  16.2 3.2 %collective-permute-start.4 = (f32[128,256]{1,0:T(8,128)S(1)}, f32[128,256]{1,0:T(8,128)S(1)}, u32[]{:S(2)}, u32[]{:S(2)}) collective-permute-start(f32[128,256]{1,0:T(8,128)S(1)} %add.37), channel_id=1, source_target_pairs={{0,48},{2,50},{4,52},{6,54},{8,24},{10,26},{12,28},{14,30},{1,193}... | collective-permute-start | bytes 393224 | tf_op jit(solution)/shard_map/ppermute | solution.py:61
  19.4 6.0 %collective-permute-start.5 = (f32[128,256]{1,0:T(8,128)S(1)}, f32[128,256]{1,0:T(8,128)S(1)}, u32[]{:S(2)}, u32[]{:S(2)}) collective-permute-start(f32[128,256]{1,0:T(8,128)S(1)} %add.38), channel_id=1, source_target_pairs={{0,56},{2,58},{4,60},{6,62},{8,16},{10,18},{12,20},{14,22},{48,40}... | collective-permute-start | bytes 393224 | tf_op jit(solution)/shard_map/ppermute | solution.py:61
  25.5 3.4 %collective-permute-start.6 = (f32[128,256]{1,0:T(8,128)S(1)}, f32[128,256]{1,0:T(8,128)S(1)}, u32[]{:S(2)}, u32[]{:S(2)}) collective-permute-start(f32[128,256]{1,0:T(8,128)S(1)} %add.39), channel_id=1, source_target_pairs={{0,64},{2,66},{4,68},{6,70},{8,72},{10,74},{12,76},{14,78},{16,80}... | collective-permute-start | bytes 393224 | tf_op jit(solution)/shard_map/ppermute | solution.py:61
  28.9 3.2 %collective-permute-start.7 = (f32[128,256]{1,0:T(8,128)S(1)}, f32[128,256]{1,0:T(8,128)S(1)}, u32[]{:S(2)}, u32[]{:S(2)}) collective-permute-start(f32[128,256]{1,0:T(8,128)S(1)} %add.40), channel_id=1, source_target_pairs={{0,192},{2,194},{4,196},{6,198},{8,200},{10,202},{12,204},{14,206}... | collective-permute-start | bytes 393224 | tf_op jit(solution)/shard_map/ppermute | solution.py:61
  32.2 18.6 %collective-permute-start.10 = (f32[128,256]{1,0:T(8,128)S(1)}, f32[128,256]{1,0:T(8,128)S(1)}, u32[]{:S(2)}, u32[]{:S(2)}) collective-permute-start(f32[128,256]{1,0:T(8,128)S(1)} %add.41), channel_id=1, source_target_pairs={{0,2},{1,3},{2,4},{3,5},{4,6},{5,7},{6,0},{7,1},{8,10},{9,11},{10,... | collective-permute-start | bytes 393224 | tf_op jit(solution)/shard_map/ppermute | solution.py:61
  32.3 18.5 %collective-permute-start.9 = (f32[128,256]{1,0:T(8,128)S(1)}, f32[128,256]{1,0:T(8,128)S(1)}, u32[]{:S(2)}, u32[]{:S(2)}) collective-permute-start(f32[128,256]{1,0:T(8,128)S(1)} %add.41), channel_id=1, source_target_pairs={{0,4},{1,5},{2,6},{3,7},{4,0},{5,1},{6,2},{7,3},{8,12},{9,13},{10,... | collective-permute-start | bytes 393224 | tf_op jit(solution)/shard_map/ppermute | solution.py:61
  35.9 14.8 %collective-permute-start.8 = (f32[128,256]{1,0:T(8,128)S(1)}, f32[128,256]{1,0:T(8,128)S(1)}, u32[]{:S(2)}, u32[]{:S(2)}) collective-permute-start(f32[128,256]{1,0:T(8,128)S(1)} %add.41), channel_id=1, source_target_pairs={{0,6},{1,7},{2,0},{3,1},{4,2},{5,3},{6,4},{7,5},{8,14},{9,15},{10,... | collective-permute-start | bytes 393224 | tf_op jit(solution)/shard_map/ppermute | solution.py:61
  37.9 14.1 %collective-permute-start.15 = (f32[64,256]{1,0:T(8,128)S(1)}, f32[64,256]{1,0:T(8,128)S(1)}, u32[]{:S(2)}, u32[]{:S(2)}) collective-permute-start(f32[64,256]{1,0:T(8,128)S(1)} %get-tuple-element.51), channel_id=1, source_target_pairs={{0,0},{1,32},{2,8},{3,40},{4,16},{5,48},{6,24},{7,56},{8,1},{9,33}... | collective-permute-start | bytes 196616 | tf_op jit(solution)/shard_map/ppermute | solution.py:61
  50.8 9.6 %collective-permute-start.11 = (f32[4,128,256]{2,1,0:T(8,128)S(1)}, f32[4,128,256]{2,1,0:T(8,128)S(1)}, u32[]{:S(2)}, u32[]{:S(2)}) collective-permute-start(f32[4,128,256]{2,1,0:T(8,128)S(1)} %pad_maximum_fusion.mine_ref), channel_id=1, source_target_pairs={{0,1},{1,0},{2,3},{3,2},{4,5},{5,4},{6,7},{7,6},{8,9},{9,8},{10,11... | collective-permute-start | bytes 1572872 | tf_op jit(solution)/shard_map/ppermute | solution.py:61
  52.0 4.9 %collective-permute-start.16 = (f32[64,256]{1,0:T(8,128)S(1)}, f32[64,256]{1,0:T(8,128)S(1)}, u32[]{:S(2)}, u32[]{:S(2)}) collective-permute-start(f32[64,256]{1,0:T(8,128)S(1)} %collective-permute-done.15), channel_id=1, source_target_pairs={{0,8},{1,9},{2,10},{3,11},{4,12},{5,13},{6,14},{7,15},{8,16},{9,17... | collective-permute-start | bytes 196616 | tf_op jit(solution)/shard_map/ppermute | solution.py:61
  52.1 5.0 %collective-permute-start.17 = (f32[64,256]{1,0:T(8,128)S(1)}, f32[64,256]{1,0:T(8,128)S(1)}, u32[]{:S(2)}, u32[]{:S(2)}) collective-permute-start(f32[64,256]{1,0:T(8,128)S(1)} %collective-permute-done.15), channel_id=1, source_target_pairs={{0,56},{1,57},{2,58},{3,59},{4,60},{5,61},{6,62},{7,63},{8,0},{9,1... | collective-permute-start | bytes 196616 | tf_op jit(solution)/shard_map/ppermute | solution.py:61
  56.9 12.7 %collective-permute-start.19 = (f32[2,64,256]{2,1,0:T(8,128)S(1)}, f32[2,64,256]{2,1,0:T(8,128)S(1)}, u32[]{:S(2)}, u32[]{:S(2)}) collective-permute-start(f32[2,64,256]{2,1,0:T(8,128)S(1)} %pad_maximum_fusion.2), channel_id=1, source_target_pairs={{0,40},{1,41},{2,42},{3,43},{4,44},{5,45},{6,46},{7,47},{8,48},{9,... | collective-permute-start | bytes 393224 | tf_op jit(solution)/shard_map/ppermute | solution.py:61
  57.0 12.6 %collective-permute-start.18 = (f32[3,64,256]{2,1,0:T(8,128)S(1)}, f32[3,64,256]{2,1,0:T(8,128)S(1)}, u32[]{:S(2)}, u32[]{:S(2)}) collective-permute-start(f32[3,64,256]{2,1,0:T(8,128)S(1)} %pad_maximum_fusion.1), channel_id=1, source_target_pairs={{0,24},{1,25},{2,26},{3,27},{4,28},{5,29},{6,30},{7,31},{8,32},{9,... | collective-permute-start | bytes 589832 | tf_op jit(solution)/shard_map/ppermute | solution.py:61
  69.7 22.4 %collective-permute-start.21 = (f32[8,64,256]{2,1,0:T(8,128)S(1)}, f32[8,64,256]{2,1,0:T(8,128)S(1)}, u32[]{:S(2)}, u32[]{:S(2)}) collective-permute-start(f32[8,64,256]{2,1,0:T(8,128)S(1)} %constant_dynamic-update-slice_fusion.own_ref), channel_id=1, source_target_pairs={{0,64},{1,65},{2,66},{3,67},{4,68},{5,69},{6,70},{7,71},{8,72},{9,... | collective-permute-start | bytes 1572872 | tf_op jit(solution)/shard_map/ppermute | solution.py:61
  70.8 21.3 %collective-permute-start.20 = (f32[8,64,256]{2,1,0:T(8,128)S(1)}, f32[8,64,256]{2,1,0:T(8,128)S(1)}, u32[]{:S(2)}, u32[]{:S(2)}) collective-permute-start(f32[8,64,256]{2,1,0:T(8,128)S(1)} %constant_dynamic-update-slice_fusion.own_ref), channel_id=1, source_target_pairs={{0,192},{1,193},{2,194},{3,195},{4,196},{5,197},{6,198},{7,199},{8... | collective-permute-start | bytes 1572872 | tf_op jit(solution)/shard_map/ppermute | solution.py:61
  72.4 7.0 %collective-permute-start.12 = (f32[256,256]{1,0:T(8,128)S(1)}, f32[256,256]{1,0:T(8,128)S(1)}, u32[]{:S(2)}, u32[]{:S(2)}) collective-permute-start(f32[256,256]{1,0:T(8,128)S(1)} %slice_select_fusion), channel_id=1, source_target_pairs={{0,2},{1,3},{8,10},{9,11},{16,18},{17,19},{24,26},{25,27},{32,34},... | collective-permute-start | bytes 786440 | tf_op jit(solution)/shard_map/ppermute | solution.py:61
  79.5 5.9 %collective-permute-start.13 = (f32[256,256]{1,0:T(8,128)S(1)}, f32[256,256]{1,0:T(8,128)S(1)}, u32[]{:S(2)}, u32[]{:S(2)}) collective-permute-start(f32[256,256]{1,0:T(8,128)S(1)} %add.42), channel_id=1, source_target_pairs={{0,6},{2,4},{1,7},{3,5},{8,14},{10,12},{9,15},{11,13},{16,22},{18,... | collective-permute-start | bytes 786440 | tf_op jit(solution)/shard_map/ppermute | solution.py:61
  85.5 13.6 %collective-permute-start.14 = (f32[256,256]{1,0:T(8,128)S(1)}, f32[256,256]{1,0:T(8,128)S(1)}, u32[]{:S(2)}, u32[]{:S(2)}) collective-permute-start(f32[256,256]{1,0:T(8,128)S(1)} %add.43.row_ref), channel_id=1, source_target_pairs={{0,1},{1,0},{2,3},{3,2},{4,5},{5,4},{6,7},{7,6},{8,9},{9,8},{10,11... | collective-permute-start | bytes 786440 | tf_op jit(solution)/shard_map/ppermute | solution.py:61
  92.1 9.1 %collective-permute-start.22 = (f32[4,64,256]{2,1,0:T(8,128)S(1)}, f32[4,64,256]{2,1,0:T(8,128)S(1)}, u32[]{:S(2)}, u32[]{:S(2)}) collective-permute-start(f32[4,64,256]{2,1,0:T(8,128)S(1)} %slice.32), channel_id=1, source_target_pairs={{0,64},{1,65},{2,66},{3,67},{4,68},{5,69},{6,70},{7,71},{8,72},{9,... | collective-permute-start | bytes 786440 | tf_op jit(solution)/shard_map/ppermute | solution.py:61
  92.7 7.6 %collective-permute-start.23 = (f32[4,64,256]{2,1,0:T(8,128)S(1)}, f32[4,64,256]{2,1,0:T(8,128)S(1)}, u32[]{:S(2)}, u32[]{:S(2)}) collective-permute-start(f32[4,64,256]{2,1,0:T(8,128)S(1)} %slice.33), channel_id=1, source_target_pairs={{0,192},{1,193},{2,194},{3,195},{4,196},{5,197},{6,198},{7,199},{8... | collective-permute-start | bytes 786440 | tf_op jit(solution)/shard_map/ppermute | solution.py:61
  (2 other events, 40.8 us)
